TPU v7x, 32 devices: a whole 2x2x4 slice. The times are simulated.
32 devices in a mesh: batch: 4 (over z), dp: 4 (over y, x), narrow: 2 (over core).
Axes of the slice: x: 2, y: 2, z: 4, core: 2. Of those that a mesh axis runs over, the one named last changes fastest.
Arguments:
- tokens: bfloat16 [36864, 1024], P(('batch', 'dp', 'narrow')), may hold values from -6 to 6
- row_kind: int32 [32], P(('batch', 'dp', 'narrow')), may hold values 0 or 1
- text_length: int32 [32, 3], P(('batch', 'dp', 'narrow')), may hold values from 1 to 128, as said below
- gain_attn: bfloat16 [1024], P(('dp', 'narrow')), may hold values from 0.099609375 to 1.8984375
- position_bias_table: bfloat16 [512], P(('dp', 'narrow')), may hold values from -4 to 4
- weight_query: bfloat16 [1024, 1024], P(('dp', 'narrow')), may hold values from -0.09375 to 0.09375
- weight_key: bfloat16 [1024, 1024], P(('dp', 'narrow')), may hold values from -0.09375 to 0.09375
- weight_value: bfloat16 [1024, 1024], P(('dp', 'narrow')), may hold values from -0.1875 to 0.1875
- weight_out: bfloat16 [1024, 1024], P(('dp', 'narrow')), may hold values from -0.5 to 0.5
- gain_ffn: bfloat16 [1024], P(('dp', 'narrow')), may hold values from 0.099609375 to 1.8984375
- weight_gate: bfloat16 [1024, 2816], P(('dp', 'narrow')), may hold values from -0.1875 to 0.1875
- weight_up: bfloat16 [1024, 2816], P(('dp', 'narrow')), may hold values from -0.1875 to 0.1875
- weight_down: bfloat16 [2816, 1024], P(('dp', 'narrow')), may hold values from -0.109375 to 0.109375
- cotangent: bfloat16 [36864, 1024], P(('batch', 'dp', 'narrow')), may hold values from -6 to 6
Outputs:
- output: bfloat16 [36864, 1024], P(('batch', 'dp', 'narrow'))
- grad_tokens: float32 [36864, 1024], P(('batch', 'dp', 'narrow'))
- grad_gain_attn: float32 [1024], P(('dp', 'narrow'))
- grad_bias_table: float32 [512], P(('dp', 'narrow'))
- grad_weight_query: float32 [1024, 1024], P(('dp', 'narrow'))
- grad_weight_key: float32 [1024, 1024], P(('dp', 'narrow'))
- grad_weight_value: float32 [1024, 1024], P(('dp', 'narrow'))
- output_weight_gradient: float32 [1024, 1024], P(('dp', 'narrow'))
- grad_gain_ffn: float32 [1024], P(('dp', 'narrow'))
- grad_weight_gate: float32 [1024, 2816], P(('dp', 'narrow'))
- grad_weight_up: float32 [1024, 2816], P(('dp', 'narrow'))
- grad_weight_down: float32 [2816, 1024], P(('dp', 'narrow'))
Inputs may be any that keep to these rules, and one draw needn't show every extreme that they name: `row_kind`: 0: the row holds one image of 1024 patches and its text; 1: three images of 256 patches, each followed by its text. `text_length`: live text tokens after each image of a row, in order; a row of kind 0 uses only the first entry.
All inputs are finite; a program needn't handle non-finite values. No bound on the sum of `row_kind` on one device may be relied on, other than what follows from the above.
Results may differ from a plain program's by a relative error of at most 0.018.
Values may be sent and summed in bfloat16 or wider, within the bound.
A program may use at most 256 MiB of HBM per device.

v0:
```python
import jax
import jax.numpy as jnp
from jax import lax
from jax.sharding import PartitionSpec as P

HEADS = 16
HEAD_DIM = 64
BUCKETS = 32
PATCH_SHORT = 256
TEXT = 128
PATCH_LONG = 1024
ROW_LEN = 1152


EPS = 1e-06
THRESHOLDS = (12, 16, 23, 32, 46, 64, 91)


def bucket_of(offsets):
    distance = jnp.abs(offsets)
    coarse = jnp.full_like(distance, BUCKETS // 4)
    for bound_value in THRESHOLDS:
        coarse = coarse + (distance >= bound_value).astype(jnp.int32)
    near_mask = distance < BUCKETS // 4
    return jnp.where(near_mask, distance, coarse) + BUCKETS // 2 * (offsets > 0).astype(jnp.int32)


def block_onehot(row_start, half_rows, length):
    query_pos = row_start + jnp.arange(half_rows, dtype=jnp.int32)
    key_pos = jnp.arange(length, dtype=jnp.int32)
    ids_block = bucket_of(key_pos[None, :] - query_pos[:, None])
    return (jnp.arange(BUCKETS, dtype=jnp.int32)[:, None, None] == ids_block[None]).astype(
        jnp.bfloat16
    )


def row_layout(row_kind, text_length, length):
    positions = jnp.arange(length, dtype=jnp.int32)
    span_size = PATCH_SHORT + TEXT
    segment = row_kind[:, None] * (positions[None, :] // span_size)
    offsets = positions[None, :] - segment * span_size
    image_len = PATCH_LONG - (PATCH_LONG - PATCH_SHORT) * row_kind
    live_text = jnp.zeros_like(segment)
    for slot_index in range(3):
        live_text = live_text + jnp.where(
            segment == slot_index, text_length[:, slot_index : slot_index + 1], 0
        )
    valid_mask = offsets < image_len[:, None] + live_text
    return (segment, valid_mask)


def rms_norm(inputs, gain):
    return inputs * lax.rsqrt(jnp.mean(inputs * inputs, axis=-1, keepdims=True) + EPS) * gain


def gated(gate_in, up_in):
    return jax.nn.gelu(gate_in, approximate=True) * up_in


def product(left, right):
    return jnp.dot(left, right, preferred_element_type=jnp.float32)


def contract_rows(left, right):
    return lax.dot_general(
        left, right, (((0,), (0,)), ((), ())), preferred_element_type=jnp.float32
    )


def contract_cols(left, right):
    return lax.dot_general(
        left, right, (((1,), (1,)), ((), ())), preferred_element_type=jnp.float32
    )


def block_scores(
    query_block,
    key_group,
    bias_table_slice,
    indicator_block,
    row_start,
    half_rows,
    seg_row,
    valid_row,
):
    raw_scores = jnp.einsum(
        "qhd,khd->hqk", query_block, key_group, preferred_element_type=jnp.float32
    )
    raw_scores = raw_scores + jnp.einsum(
        "id,dfp->ifp", bias_table_slice, indicator_block, preferred_element_type=jnp.float32
    )
    allowed = (seg_row[row_start : row_start + half_rows, None] == seg_row[None, :]) & valid_row[
        None, :
    ]
    return jnp.where(allowed[None], raw_scores, -1e30)


def attend_forward(queries, key_rows, value_rows, segment, valid_mask, table_matrix, onehots):
    row_count, length = segment.shape
    feature_width = queries.shape[1]
    group_heads = 4
    group_width = group_heads * HEAD_DIM
    groups = HEADS // group_heads
    half_rows = length // 2

    def one_row(carry_value, row_items):
        query_row, key_row, value_row, seg_row, valid_row = row_items

        def one_group(inner_carry, group_index):
            column = group_index * group_width
            query_group = lax.dynamic_slice_in_dim(query_row, column, group_width, 1).reshape(
                length, group_heads, HEAD_DIM
            )
            key_group = lax.dynamic_slice_in_dim(key_row, column, group_width, 1).reshape(
                length, group_heads, HEAD_DIM
            )
            value_group = lax.dynamic_slice_in_dim(value_row, column, group_width, 1).reshape(
                length, group_heads, HEAD_DIM
            )
            bias_table_slice = lax.dynamic_slice_in_dim(
                table_matrix, group_index * group_heads, group_heads, 0
            )
            pieces = []
            totals = []
            for block_index, row_start in enumerate((0, half_rows)):
                scores = block_scores(
                    query_group[row_start : row_start + half_rows],
                    key_group,
                    bias_table_slice,
                    onehots[block_index],
                    row_start,
                    half_rows,
                    seg_row,
                    valid_row,
                )
                row_peak = jnp.max(scores, axis=-1, keepdims=True)
                log_total = row_peak + jnp.log(
                    jnp.sum(jnp.exp(scores - row_peak), axis=-1, keepdims=True)
                )
                soft_weights = jnp.exp(scores - log_total).astype(jnp.bfloat16)
                pieces.append(
                    jnp.einsum(
                        "hqk,khd->qhd",
                        soft_weights,
                        value_group,
                        preferred_element_type=jnp.float32,
                    )
                )
                totals.append(log_total[:, :, 0])
            return (
                inner_carry,
                (
                    jnp.concatenate(pieces, 0).reshape(length, group_width),
                    jnp.concatenate(totals, 1),
                ),
            )

        _, (group_out, group_totals) = lax.scan(
            one_group, carry_value, jnp.arange(groups, dtype=jnp.int32)
        )
        row_out = jnp.moveaxis(group_out, 0, 1).reshape(length, feature_width)
        return (carry_value, (row_out, group_totals.reshape(HEADS, length)))

    _, (outputs, log_totals) = lax.scan(
        one_row,
        jnp.float32(0.0),
        (
            queries.reshape(row_count, length, feature_width),
            key_rows.reshape(row_count, length, feature_width),
            value_rows.reshape(row_count, length, feature_width),
            segment,
            valid_mask,
        ),
    )
    return (outputs.reshape(row_count * length, feature_width), log_totals)


def attend_backward(
    queries, key_rows, value_rows, grad_out, log_totals, segment, valid_mask, table_matrix, onehots
):
    row_count, length = segment.shape
    feature_width = queries.shape[1]
    group_heads = 4
    group_width = group_heads * HEAD_DIM
    groups = HEADS // group_heads
    half_rows = length // 2

    def one_row(table_total, row_items):
        query_row, key_row, value_row, grad_row, total_row, seg_row, valid_row = row_items

        def one_group(inner_carry, group_index):
            column = group_index * group_width
            query_group = lax.dynamic_slice_in_dim(query_row, column, group_width, 1).reshape(
                length, group_heads, HEAD_DIM
            )
            key_group = lax.dynamic_slice_in_dim(key_row, column, group_width, 1).reshape(
                length, group_heads, HEAD_DIM
            )
            value_group = lax.dynamic_slice_in_dim(value_row, column, group_width, 1).reshape(
                length, group_heads, HEAD_DIM
            )
            grad_group = lax.dynamic_slice_in_dim(grad_row, column, group_width, 1).reshape(
                length, group_heads, HEAD_DIM
            )
            total_group = lax.dynamic_slice_in_dim(
                total_row, group_index * group_heads, group_heads, 0
            )
            bias_table_slice = lax.dynamic_slice_in_dim(
                table_matrix, group_index * group_heads, group_heads, 0
            )
            key_grad = jnp.zeros((length, group_heads, HEAD_DIM), jnp.float32)
            value_grad = jnp.zeros((length, group_heads, HEAD_DIM), jnp.float32)
            table_part = jnp.zeros((group_heads, BUCKETS), jnp.float32)
            query_pieces = []
            for block_index, row_start in enumerate((0, half_rows)):
                query_block = query_group[row_start : row_start + half_rows]
                grad_block = grad_group[row_start : row_start + half_rows]
                scores = block_scores(
                    query_block,
                    key_group,
                    bias_table_slice,
                    onehots[block_index],
                    row_start,
                    half_rows,
                    seg_row,
                    valid_row,
                )
                soft_weights = jnp.exp(
                    scores - total_group[:, row_start : row_start + half_rows, None]
                )
                weights_low = soft_weights.astype(jnp.bfloat16)
                grad_probs = jnp.einsum(
                    "qhd,khd->hqk", grad_block, value_group, preferred_element_type=jnp.float32
                )
                inner_sum = jnp.sum(soft_weights * grad_probs, axis=-1, keepdims=True)
                grad_scores = (soft_weights * (grad_probs - inner_sum)).astype(jnp.bfloat16)
                query_pieces.append(
                    jnp.einsum(
                        "hqk,khd->qhd", grad_scores, key_group, preferred_element_type=jnp.float32
                    )
                )
                key_grad = key_grad + jnp.einsum(
                    "hqk,qhd->khd", grad_scores, query_block, preferred_element_type=jnp.float32
                )
                value_grad = value_grad + jnp.einsum(
                    "hqk,qhd->khd", weights_low, grad_block, preferred_element_type=jnp.float32
                )
                table_part = table_part + jnp.einsum(
                    "wle,cle->wc",
                    grad_scores,
                    onehots[block_index],
                    preferred_element_type=jnp.float32,
                )
            return (
                inner_carry,
                (
                    jnp.concatenate(query_pieces, 0).reshape(length, group_width),
                    key_grad.reshape(length, group_width),
                    value_grad.reshape(length, group_width),
                    table_part,
                ),
            )

        _, (grad_query_g, grad_key_g, grad_value_g, table_groups) = lax.scan(
            one_group, jnp.float32(0.0), jnp.arange(groups, dtype=jnp.int32)
        )
        query_part = jnp.moveaxis(grad_query_g, 0, 1).reshape(length, feature_width)
        key_part = jnp.moveaxis(grad_key_g, 0, 1).reshape(length, feature_width)
        value_part = jnp.moveaxis(grad_value_g, 0, 1).reshape(length, feature_width)
        return (
            table_total + table_groups.reshape(HEADS, BUCKETS),
            (query_part, key_part, value_part),
        )

    table_start = jnp.zeros((HEADS, BUCKETS), jnp.float32)
    table_total, (grad_queries, grad_keys, grad_values) = lax.scan(
        one_row,
        table_start,
        (
            queries.reshape(row_count, length, feature_width),
            key_rows.reshape(row_count, length, feature_width),
            value_rows.reshape(row_count, length, feature_width),
            grad_out.reshape(row_count, length, feature_width),
            log_totals,
            segment,
            valid_mask,
        ),
    )
    total_rows = row_count * length
    return (
        grad_queries.reshape(total_rows, feature_width),
        grad_keys.reshape(total_rows, feature_width),
        grad_values.reshape(total_rows, feature_width),
        table_total,
    )


def per_device(
    tokens,
    row_kind,
    text_length,
    gain_attn,
    position_bias_table,
    weight_query,
    weight_key,
    weight_value,
    weight_out,
    gain_ffn,
    weight_gate,
    weight_up,
    weight_down,
    cotangent,
):
    length = ROW_LEN
    half_rows = length // 2
    segment, valid_mask = row_layout(row_kind, text_length, length)
    onehots = (block_onehot(0, half_rows, length), block_onehot(half_rows, half_rows, length))
    gain_one, table_rel, query_w, key_w, value_w, out_w = (
        lax.all_gather(gain_attn, ("dp", "narrow"), axis=0, tiled=True),
        lax.all_gather(position_bias_table, ("dp", "narrow"), axis=0, tiled=True),
        lax.all_gather(weight_query, ("dp", "narrow"), axis=0, tiled=True),
        lax.all_gather(weight_key, ("dp", "narrow"), axis=0, tiled=True),
        lax.all_gather(weight_value, ("dp", "narrow"), axis=0, tiled=True),
        lax.all_gather(weight_out, ("dp", "narrow"), axis=0, tiled=True),
    )
    inputs = tokens.astype(jnp.float32)
    gain_one_f = gain_one.astype(jnp.float32)
    normalized_rows = rms_norm(inputs, gain_one_f).astype(jnp.bfloat16)
    queries = product(normalized_rows, query_w).astype(jnp.bfloat16)
    key_rows = product(normalized_rows, key_w).astype(jnp.bfloat16)
    value_rows = product(normalized_rows, value_w).astype(jnp.bfloat16)
    table_matrix = table_rel.reshape(HEADS, BUCKETS)
    attended, log_totals = attend_forward(
        queries, key_rows, value_rows, segment, valid_mask, table_matrix, onehots
    )
    context = attended.astype(jnp.bfloat16)
    residual_stream = inputs + product(context, out_w)
    gain_two, gate_w, upper_w, down_w = (
        lax.all_gather(gain_ffn, ("dp", "narrow"), axis=0, tiled=True),
        lax.all_gather(weight_gate, ("dp", "narrow"), axis=0, tiled=True),
        lax.all_gather(weight_up, ("dp", "narrow"), axis=0, tiled=True),
        lax.all_gather(weight_down, ("dp", "narrow"), axis=0, tiled=True),
    )
    gain_two_f = gain_two.astype(jnp.float32)
    normed_ffn = rms_norm(residual_stream, gain_two_f).astype(jnp.bfloat16)
    gate_pre = product(normed_ffn, gate_w)
    up_pre = product(normed_ffn, upper_w)
    hidden = gated(gate_pre, up_pre).astype(jnp.bfloat16)
    output = (residual_stream + product(hidden, down_w)).astype(jnp.bfloat16)
    gain_two, gate_w, upper_w, down_w = (
        lax.all_gather(gain_ffn, ("dp", "narrow"), axis=0, tiled=True),
        lax.all_gather(weight_gate, ("dp", "narrow"), axis=0, tiled=True),
        lax.all_gather(weight_up, ("dp", "narrow"), axis=0, tiled=True),
        lax.all_gather(weight_down, ("dp", "narrow"), axis=0, tiled=True),
    )
    gain_two_f = gain_two.astype(jnp.float32)
    grad_output = cotangent.astype(jnp.float32)
    grad_down = contract_rows(hidden, cotangent)
    grad_hidden = contract_cols(cotangent, down_w)
    _, gate_pull = jax.vjp(gated, gate_pre, up_pre)
    grad_gate_pre, grad_up_pre = gate_pull(grad_hidden)
    grad_gate_low = grad_gate_pre.astype(jnp.bfloat16)
    grad_up_low = grad_up_pre.astype(jnp.bfloat16)
    grad_gate_w = contract_rows(normed_ffn, grad_gate_low)
    grad_up_w = contract_rows(normed_ffn, grad_up_low)
    grad_normed_ffn = contract_cols(grad_gate_low, gate_w) + contract_cols(grad_up_low, upper_w)
    _, norm_pull = jax.vjp(rms_norm, residual_stream, gain_two_f)
    grad_residual_part, grad_gain_two = norm_pull(grad_normed_ffn)
    grad_residual = grad_output + grad_residual_part
    ffn_shards = (
        lax.psum_scatter(grad_gain_two, ("dp", "narrow"), scatter_dimension=0, tiled=True),
        lax.psum_scatter(grad_gate_w, ("dp", "narrow"), scatter_dimension=0, tiled=True),
        lax.psum_scatter(grad_up_w, ("dp", "narrow"), scatter_dimension=0, tiled=True),
        lax.psum_scatter(grad_down, ("dp", "narrow"), scatter_dimension=0, tiled=True),
    )
    ffn_sums = (
        lax.psum(ffn_shards[0].astype(jnp.bfloat16), "batch").astype(jnp.float32),
        lax.psum(ffn_shards[1].astype(jnp.bfloat16), "batch").astype(jnp.float32),
        lax.psum(ffn_shards[2].astype(jnp.bfloat16), "batch").astype(jnp.float32),
        lax.psum(ffn_shards[3].astype(jnp.bfloat16), "batch").astype(jnp.float32),
    )
    gain_one, table_rel, query_w, key_w, value_w, out_w = (
        lax.all_gather(gain_attn, ("dp", "narrow"), axis=0, tiled=True),
        lax.all_gather(position_bias_table, ("dp", "narrow"), axis=0, tiled=True),
        lax.all_gather(weight_query, ("dp", "narrow"), axis=0, tiled=True),
        lax.all_gather(weight_key, ("dp", "narrow"), axis=0, tiled=True),
        lax.all_gather(weight_value, ("dp", "narrow"), axis=0, tiled=True),
        lax.all_gather(weight_out, ("dp", "narrow"), axis=0, tiled=True),
    )
    gain_one_f = gain_one.astype(jnp.float32)
    table_matrix = table_rel.reshape(HEADS, BUCKETS)
    grad_attn_low = grad_residual.astype(jnp.bfloat16)
    grad_out_w = contract_rows(context, grad_attn_low)
    grad_context = contract_cols(grad_attn_low, out_w).astype(jnp.bfloat16)
    grad_queries, grad_keys, grad_values, table_total = attend_backward(
        queries,
        key_rows,
        value_rows,
        grad_context,
        log_totals,
        segment,
        valid_mask,
        table_matrix,
        onehots,
    )
    grad_queries_low = grad_queries.astype(jnp.bfloat16)
    grad_keys_low = grad_keys.astype(jnp.bfloat16)
    grad_values_low = grad_values.astype(jnp.bfloat16)
    grad_query_w = contract_rows(normalized_rows, grad_queries_low)
    grad_key_w = contract_rows(normalized_rows, grad_keys_low)
    grad_value_w = contract_rows(normalized_rows, grad_values_low)
    grad_normed = (
        contract_cols(grad_queries_low, query_w)
        + contract_cols(grad_keys_low, key_w)
        + contract_cols(grad_values_low, value_w)
    )
    _, first_pull = jax.vjp(rms_norm, inputs, gain_one_f)
    input_gradient_share, grad_gain_one = first_pull(grad_normed)
    grad_tokens = grad_residual + input_gradient_share
    grad_table = table_total.reshape(HEADS * BUCKETS)
    attn_shards = (
        lax.psum_scatter(grad_gain_one, ("dp", "narrow"), scatter_dimension=0, tiled=True),
        lax.psum_scatter(grad_table, ("dp", "narrow"), scatter_dimension=0, tiled=True),
        lax.psum_scatter(grad_query_w, ("dp", "narrow"), scatter_dimension=0, tiled=True),
        lax.psum_scatter(grad_key_w, ("dp", "narrow"), scatter_dimension=0, tiled=True),
        lax.psum_scatter(grad_value_w, ("dp", "narrow"), scatter_dimension=0, tiled=True),
        lax.psum_scatter(grad_out_w, ("dp", "narrow"), scatter_dimension=0, tiled=True),
    )
    attn_sums = (
        lax.psum(attn_shards[0].astype(jnp.bfloat16), "batch").astype(jnp.float32),
        lax.psum(attn_shards[1].astype(jnp.bfloat16), "batch").astype(jnp.float32),
        lax.psum(attn_shards[2].astype(jnp.bfloat16), "batch").astype(jnp.float32),
        lax.psum(attn_shards[3].astype(jnp.bfloat16), "batch").astype(jnp.float32),
        lax.psum(attn_shards[4].astype(jnp.bfloat16), "batch").astype(jnp.float32),
        lax.psum(attn_shards[5].astype(jnp.bfloat16), "batch").astype(jnp.float32),
    )
    return (
        output,
        grad_tokens,
        attn_sums[0],
        attn_sums[1],
        attn_sums[2],
        attn_sums[3],
        attn_sums[4],
        attn_sums[5],
        ffn_sums[0],
        ffn_sums[1],
        ffn_sums[2],
        ffn_sums[3],
    )


def solution(mesh):
    placed = (
        P(("batch", "dp", "narrow"), None),
        P(("batch", "dp", "narrow")),
        P(("batch", "dp", "narrow"), None),
        P(("dp", "narrow")),
        P(("dp", "narrow")),
        P(("dp", "narrow"), None),
        P(("dp", "narrow"), None),
        P(("dp", "narrow"), None),
        P(("dp", "narrow"), None),
        P(("dp", "narrow")),
        P(("dp", "narrow"), None),
        P(("dp", "narrow"), None),
        P(("dp", "narrow"), None),
        P(("batch", "dp", "narrow"), None),
    )
    return jax.shard_map(
        per_device,
        mesh=mesh,
        in_specs=placed,
        out_specs=(
            P(("batch", "dp", "narrow"), None),
            P(("batch", "dp", "narrow"), None),
            P(("dp", "narrow")),
            P(("dp", "narrow")),
            P(("dp", "narrow"), None),
            P(("dp", "narrow"), None),
            P(("dp", "narrow"), None),
            P(("dp", "narrow"), None),
            P(("dp", "narrow")),
            P(("dp", "narrow"), None),
            P(("dp", "narrow"), None),
            P(("dp", "narrow"), None),
        ),
        check_vma=False,
    )
```

profile of v0, /device:TPU:0, one launch (start us, length us, event | category | flops | bytes accessed | tf_op | source)
XLA Modules:
  0.0 1453.4 jit_solution(16543961559594165222)
XLA Ops:
  15.5 15.3 %all-reduce = bf16[512]{0:T(512)(128)(2,1)S(1)} all-reduce(bf16[512]{0:T(512)(128)(2,1)S(1)} %dynamic-update-slice), channel_id=1, replica_groups=mesh['batch'=4,'dp'=4,'narrow'=2] {'dp','narrow'}, use_global_device_ids=true, to_apply=%add | all-reduce | flops 512 | bytes 2048
  32.3 7.6 all-gather
  40.0 8.8 all-gather.1
  57.6 6.9 fusion.112
  80.5 18.1 %copy.58 = bf16[1152,1024]{0,1:T(8,128)(2,1)} copy(bf16[1152,1024]{1,0:T(8,128)(2,1)} %convolution_convert_fusion.1) | data formatting | bytes 4718592
  112.1 169.4 %while.53 = (s32[]{:T(128)}, bf16[4,1152,256]{1,2,0:T(8,128)(2,1)}, f32[4,4,1152]{2,1,0:T(4,128)}, s32[4]{0:T(128)S(1)}, bf16[1152,1024]{0,1:T(8,128)(2,1)}, /*i...) while((s32[]{:T(128)}, bf16[4,1152,256]{1,2,0:T(8,128)(2,1)}, ...), condition=%wide.region_6.7_spmd.clone, body=%wide.region_1.6_spmd.clone.sunk | while | flops 1824644736 | bytes 142631696 | solution.py:158
  137.1 7.2 fusion.295
  179.3 7.1 fusion.295
  221.4 7.1 fusion.295
  263.9 7.2 fusion.295
  282.5 6.3 multiply_reduce_fusion.4
  292.8 12.1 fusion.160
  304.9 13.2 fusion.159
  318.1 24.0 %multiply_convert_fusion.2 = (bf16[1152,2816]{1,0:T(8,128)(2,1)}, bf16[1152,2816]{1,0:T(8,128)(2,1)}, bf16[1152,2816]{1,0:T(8,128)(2,1)}) fusion(f32[1152,2816]{1,0:T(8,128)} %fusion.159, f32[1152,2816]{1,0:T(8,128)} %fusion.160, bf16[1152,1024]{1,0:T(8,128)(2,1)S(1)} %copy-done.14, bf16[2816,1024]{1,0:T(8,128)(2,1)} %all-gather.22.cloned.1.call-done), kind=kOutput, calls=%fused_computation.120 | convolution fusion | flops 6728122368 | bytes 53542912 | tf_op jit(solution)/shard_map/dot_general | solution.py:71
  342.0 11.7 fusion.161
  353.8 11.7 multiply_reduce_fusion.2
  376.2 6.3 convolution_convert_fusion
  387.3 478.0 %while.54 = (s32[]{:T(128)}, bf16[4,1152,256]{1,2,0:T(8,128)(2,1)}, bf16[4,1152,256]{1,2,0:T(8,128)(2,1)}, bf16[4,1152,256]{1,2,0:T(8,128)(2,1)}, f32[4,4,32]{2,...) while((s32[]{:T(128)}, bf16[4,1152,256]{1,2,0:T(8,128)(2,1)}, ...), condition=%wide.region_12.13_spmd.clone.clone, body=%wide.region_9.12_spmd.clone.clone.sunk | while | flops 4299541504 | bytes 301815008 | solution.py:264
  420.8 8.9 fusion.331
  429.6 14.0 multiply_reduce_fusion.8
  443.7 7.7 multiply_convert_fusion.8
  451.4 13.5 fusion.335
  467.6 9.0 fusion.328
  476.6 12.0 multiply_reduce_fusion.7
  504.6 11.8 fusion.336
  536.2 8.9 fusion.331
  545.0 14.0 multiply_reduce_fusion.8
  559.1 7.7 multiply_convert_fusion.8
  566.8 13.5 fusion.335
  583.0 9.0 fusion.328
  592.0 12.0 multiply_reduce_fusion.7
  620.0 11.8 fusion.336
  651.6 8.9 fusion.331
  660.5 14.0 multiply_reduce_fusion.8
  674.5 7.7 multiply_convert_fusion.8
  682.3 13.5 fusion.335
  698.5 9.0 fusion.328
  707.5 12.0 multiply_reduce_fusion.7
  735.5 11.8 fusion.336
  767.0 8.9 fusion.331
  775.9 14.0 multiply_reduce_fusion.8
  790.0 7.7 multiply_convert_fusion.8
  797.7 13.5 fusion.335
  813.9 9.0 fusion.328
  822.9 12.0 multiply_reduce_fusion.7
  850.9 11.8 fusion.336
  865.4 7.5 fusion.145
  873.0 6.3 fusion.143
  879.4 6.4 fusion.141
  885.9 13.8 fusion.163
  899.8 13.6 fusion.162
  913.4 13.3 fusion.164
  928.0 13.4 add_convert_fusion
  945.0 34.5 %reduce-scatter.10.cloned.1.call-done = f32[128,1024]{1,0:T(8,128)} async-done(((f32[1024,1024]{1,0:T(8,128)}), f32[128,1024]{1,0:T(8,128)}) %reduce-scatter.10.cloned.1.call-update) | async-done | bytes 524304 | tf_op jit(solution)/shard_map/reduce_scatter | solution.py:425
  981.3 53.3 %reduce-scatter.12.cloned.1.call-done = f32[128,1024]{1,0:T(8,128)} async-done(((f32[1024,1024]{1,0:T(8,128)}), f32[128,1024]{1,0:T(8,128)}) %reduce-scatter.12.cloned.1.call-update) | async-done | bytes 524304 | tf_op jit(solution)/shard_map/reduce_scatter | solution.py:426
  1036.4 88.4 %reduce-scatter.18.cloned.1.call-done = f32[128,2816]{1,0:T(8,128)} async-done(((f32[1024,2816]{1,0:T(8,128)}), f32[128,2816]{1,0:T(8,128)}) %reduce-scatter.18.cloned.1.call-update) | async-done | bytes 1441808 | tf_op jit(solution)/shard_map/reduce_scatter | solution.py:373
  1127.1 88.0 %reduce-scatter.16.cloned.1.call-done = f32[128,2816]{1,0:T(8,128)} async-done(((f32[1024,2816]{1,0:T(8,128)}), f32[128,2816]{1,0:T(8,128)}) %reduce-scatter.16.cloned.1.call-update) | async-done | bytes 1441808 | tf_op jit(solution)/shard_map/reduce_scatter | solution.py:372
  1217.4 87.9 %reduce-scatter.20.cloned.1.call-done = f32[352,1024]{1,0:T(8,128)} async-done(((f32[2816,1024]{1,0:T(8,128)}), f32[352,1024]{1,0:T(8,128)}) %reduce-scatter.20.cloned.1.call-update) | async-done | bytes 1441808 | tf_op jit(solution)/shard_map/reduce_scatter | solution.py:374
  1307.7 7.4 fusion.165
  1330.2 25.0 %all-reduce.4 = (bf16[1024]{0:T(1024)(128)(2,1)S(1)}, bf16[512]{0:T(512)(128)(2,1)S(1)}, bf16[1024]{0:T(1024)(128)(2,1)S(1)}) all-reduce(f32[1024]{0:T(1024)S(1)} %get-tuple-element.481, f32[512]{0:T(512)S(1)} %reshape.469, f32[1024]{0:T(1024)S(1)} %copy-done.26), channel_id=2, replica_groups=mesh['batch'=4,'dp'=4,'narrow'=2] {'dp','narrow'}, use_global_device_ids=true, to_apply=%region_15.16.clone | all-reduce | flops 2560 | bytes 15360
  1355.3 7.1 fusion.109
  1362.4 6.1 copy.71
  1368.6 11.8 all-reduce.5
  1381.9 52.7 %all-reduce.9.cloned.1.call-done = (bf16[128,1024]{1,0:T(8,128)(2,1)}, bf16[128,1024]{1,0:T(8,128)(2,1)}, bf16[128,1024]{1,0:T(8,128)(2,1)}, bf16[128,1024]{1,0:...) async-done(((bf16[128,1024]{1,0:T(8,128)(2,1)}, bf16[128,1024]{1,0:T(8,128)(2,1)}, bf16[128,1024]{1,0:T(8,128)(2,1)}, ...) | async-done | bytes 3211280 | tf_op jit(solution)/shard_map/psum | solution.py:432
  (364 shorter events, 393.4 us)
Async XLA Ops:
  7.2 57.3 %all-gather.12.cloned.1.call-start = ((), (), s32[]{:S(2)}) async-start(), calls=%async_computation.8 | async-start | bytes 2359296 | tf_op jit(solution)/shard_map/all_gather | solution.py:321
  7.9 66.8 %all-gather.14.cloned.1.call-start = ((), (), s32[]{:S(2)}) async-start(), calls=%async_computation.9 | async-start | bytes 2359296 | tf_op jit(solution)/shard_map/all_gather | solution.py:322
  8.7 91.6 %all-gather.10.cloned.1.call-start = ((), (), s32[]{:S(2)}) async-start(), calls=%async_computation.7 | async-start | bytes 2359296 | tf_op jit(solution)/shard_map/all_gather | solution.py:323
  9.4 273.1 %all-gather.16.cloned.1.call-start = ((), (), s32[]{:S(2)}) async-start(), calls=%async_computation.10 | async-start | bytes 2359296 | tf_op jit(solution)/shard_map/all_gather | solution.py:324
  10.0 281.4 %all-gather.20.cloned.1.call-start = ((), (), s32[]{:S(2)}) async-start(), calls=%async_computation.12 | async-start | bytes 6488064 | tf_op jit(solution)/shard_map/all_gather | solution.py:341
  10.6 294.3 %all-gather.18.cloned.1.call-start = ((), (), s32[]{:S(2)}) async-start(), calls=%async_computation.11 | async-start | bytes 6488064 | tf_op jit(solution)/shard_map/all_gather | solution.py:340
  11.1 306.9 %all-gather.22.cloned.1.call-start = ((), (), s32[]{:S(2)}) async-start(), calls=%async_computation.13 | async-start | bytes 6488064 | tf_op jit(solution)/shard_map/all_gather | solution.py:342
  11.9 929.6 %reduce-scatter.14.cloned.1.call-start = ((), (), s32[]{:S(2)}) async-start(), calls=%async_computation.17 | async-start | bytes 4718592 | tf_op jit(solution)/shard_map/reduce_scatter | solution.py:427
  39.9 60.3 %copy-start.23 = (f32[8,1,128]{2,1,0:T(1,128)}, f32[8,1,128]{2,1,0:T(1,128)S(1)}, u32[]{:S(2)}) copy-start(f32[8,1,128]{2,1,0:T(1,128)S(1)} %convert_element_type.398) | copy-start | bytes 12292
  52.4 47.8 %copy-start.5 = (bf16[1152,1024]{0,1:T(8,128)(2,1)}, bf16[1152,1024]{0,1:T(8,128)(2,1)S(1)}, u32[]{:S(2)}) copy-start(bf16[1152,1024]{0,1:T(8,128)(2,1)S(1)} %copy.55) | copy-start | bytes 7077892
  53.0 11.5 copy-start.18
  53.0 47.3 %copy-start.21 = (f32[1152]{0:T(1024)}, f32[1152]{0:T(1024)S(1)}, u32[]{:S(2)}) copy-start(f32[1152]{0:T(1024)S(1)} %fusion.139) | copy-start | bytes 13828
  114.0 8.1 copy-start.10
  132.2 2.1 copy-start.2
  137.0 7.2 copy-start.1
  148.4 2.1 copy-start.3
  150.4 2.1 copy-start.4
  156.2 8.1 copy-start.10
  174.4 2.1 copy-start.2
  179.2 7.1 copy-start.1
  190.5 2.1 copy-start.3
  192.6 2.1 copy-start.4
  198.3 8.1 copy-start.10
  216.6 2.1 copy-start.2
  221.4 7.1 copy-start.1
  232.7 2.1 copy-start.3
  234.7 2.1 copy-start.4
  240.4 8.4 copy-start.10
  259.1 2.1 copy-start.2
  263.9 7.2 copy-start.1
  275.2 2.1 copy-start.3
  277.3 2.1 copy-start.4
  282.5 8.5 copy-start.20
  288.7 2.2 copy-start.7
  304.9 13.2 copy-start.14
  342.0 11.7 copy-start.30
  353.8 11.8 copy-start.9
  365.6 6.0 copy-start.13
  369.4 2.2 copy-start.8
  371.6 4.5 copy-start.28
  376.1 567.1 %reduce-scatter.8.cloned.1.call-start = ((), (), s32[]{:S(2)}) async-start(), calls=%async_computation.14 | async-start | bytes 4718592 | tf_op jit(solution)/shard_map/reduce_scatter | solution.py:424
  382.5 4.8 copy-start.25
  387.3 478.1 %copy-start.22 = (f32[1152]{0:T(1024)S(1)}, f32[1152]{0:T(1024)}, u32[]{:S(2)}) copy-start(f32[1152]{0:T(1024)} %copy-done.21) | copy-start | bytes 13828
  387.3 478.1 %copy-start.24 = (f32[8,1,128]{2,1,0:T(1,128)S(1)}, f32[8,1,128]{2,1,0:T(1,128)}, u32[]{:S(2)}) copy-start(f32[8,1,128]{2,1,0:T(1,128)} %copy-done.23) | copy-start | bytes 12292
  488.6 7.1 copy-start
  502.9 1.8 copy-start.11
  604.0 7.1 copy-start
  618.3 1.8 copy-start.11
  719.4 7.1 copy-start
  834.9 7.1 copy-start
  865.4 7.6 copy-start.6
  872.9 106.6 %reduce-scatter.10.cloned.1.call-start = ((), (), s32[]{:S(2)}) async-start(), calls=%async_computation.15 | async-start | bytes 4718592 | tf_op jit(solution)/shard_map/reduce_scatter | solution.py:425
  879.4 155.3 %reduce-scatter.12.cloned.1.call-start = ((), (), s32[]{:S(2)}) async-start(), calls=%async_computation.16 | async-start | bytes 4718592 | tf_op jit(solution)/shard_map/reduce_scatter | solution.py:426
  885.8 239.0 %reduce-scatter.18.cloned.1.call-start = ((), (), s32[]{:S(2)}) async-start(), calls=%async_computation.19 | async-start | bytes 12976128 | tf_op jit(solution)/shard_map/reduce_scatter | solution.py:373
  899.7 315.4 %reduce-scatter.16.cloned.1.call-start = ((), (), s32[]{:S(2)}) async-start(), calls=%async_computation.18 | async-start | bytes 12976128 | tf_op jit(solution)/shard_map/reduce_scatter | solution.py:372
  913.3 392.0 %reduce-scatter.20.cloned.1.call-start = ((), (), s32[]{:S(2)}) async-start(), calls=%async_computation.20 | async-start | bytes 12976128 | tf_op jit(solution)/shard_map/reduce_scatter | solution.py:374
  926.7 508.0 %all-reduce.9.cloned.1.call-start = ((), (), s32[]{:S(2)}) async-start(), calls=%async_computation.21 | async-start | bytes 6422528 | tf_op jit(solution)/shard_map/psum | solution.py:432
  1319.4 5.3 copy-start.12
  1319.4 5.3 copy-start.27
  1319.4 5.3 copy-start.29
  1324.8 5.4 copy-start.26
  1324.8 30.5 %copy-start.19 = (f32[1152]{0:T(1024)S(1)}, f32[1152]{0:T(1024)}, u32[]{:S(2)}) copy-start(f32[1152]{0:T(1024)} %copy-done.18) | copy-start | bytes 13828
  1434.6 9.6 copy-start.17
  1434.6 10.8 copy-start.16
  (3 other events, 4.9 us)
Sparse Core Ops, SparseCore 0:
  9.9 30.6 all-gather.11
  42.5 27.8 all-gather.13
  72.3 27.8 all-gather.9
  102.0 27.8 all-gather.15
  131.7 43.3 all-gather.19
  176.8 43.3 all-gather.17
  222.0 43.3 all-gather.21
  376.2 51.8 reduce-scatter.13
  873.0 51.8 reduce-scatter.7
  928.2 51.3 reduce-scatter.9
  983.3 51.3 reduce-scatter.11
  1038.0 86.7 reduce-scatter.17
  1128.3 86.7 reduce-scatter.15
  1218.5 86.7 reduce-scatter.19
  1309.2 125.3 all-reduce.8
where the time goes:
time: 1470 us; the launch traced here: 1450 us
  matrix products  656 us (45%)
  waiting for transfers between devices  411 us (28%)
  other arithmetic  148 us (10%)
  local copies, waits for them, and re-layouts  124 us (8%)
  blocking collectives  68.6 us (5%)
  loops' own time  28.1 us (2%)
  between operations  17.1 us (1%)
    dot_general x16, matrix products, block_scores(): jnp.einsum('qhd,khd->hqk', query_block, key_group, preferred_element_type...  137 us
    dot_general x16, matrix products, block_scores(): jnp.einsum('id,dfp->ifp', bias_table_slice, indicator_block, preferred_el...  124 us
    dot_general x8, matrix products, one_group(): jnp.einsum('wle,cle->wc', grad_scores, onehots[block_index], preferred_el...  101 us
    reduce_scatter x1, waiting for transfers between devices, per_device(): lax.psum_scatter(grad_up_w, ('dp', 'narrow'), scatter_dimension=0, tiled=...  88.4 us
    reduce_scatter x1, waiting for transfers between devices, per_device(): lax.psum_scatter(grad_gate_w, ('dp', 'narrow'), scatter_dimension=0, tile...  88 us
    reduce_scatter x1, waiting for transfers between devices, per_device(): lax.psum_scatter(grad_down, ('dp', 'narrow'), scatter_dimension=0, tiled=...  87.9 us
    dot_general x7, matrix products, contract_cols(): lax.dot_general(left, right, (((1,), (1,)), ((), ())), preferred_element_...  71.8 us
    dot_general x7, matrix products, contract_rows(): lax.dot_general(left, right, (((0,), (0,)), ((), ())), preferred_element_...  65.3 us
  transfers between devices with their start and end apart: 15, of which 7 were waited for; matrix products, arithmetic and copies ran while one was open for 58% of the time, Pallas kernels for 0%

commit v1 on v0

v1 whole, which is shorter than its diff:
```python
import jax
import jax.numpy as jnp
import numpy as np
from jax import lax
from jax.experimental import pallas as pl
from jax.experimental.pallas import tpu as pltpu
from jax.sharding import PartitionSpec as P

bf=jnp.bfloat16; f32=jnp.float32
T=128; L=1152; NT=L//T
NEG=-1e30
def dot(a,b): return jnp.dot(a,b,preferred_element_type=f32)
def dot_tl(a,b): return lax.dot_general(a,b,(((0,),(0,)),((),())),preferred_element_type=f32)

def fwd_kernel(q_ref,k_ref,v_ref,mask_ref,far_ref,w_ref,o_ref,e_ref,r_ref,rhs,kaug,vaug,bn,s_ref):
    @pl.when((pl.program_id(0)==0)&(pl.program_id(1)==0))
    def _():
        rhs[...]=jnp.zeros_like(rhs)
        row=lax.broadcasted_iota(jnp.int32,(128,NT*256),0)
        col=lax.broadcasted_iota(jnp.int32,(128,NT*256),1)
        rhs[128:256,:]=(row==col//128).astype(f32).astype(bf)
        vaug[:,128:256]=jnp.ones((L,128),bf)
    qT=q_ref[...].T
    for i in range(NT):
        rhs[0:64,256*i:256*i+128]=qT[0:64,128*i:128*i+128]
        rhs[64:128,256*i+128:256*i+256]=qT[64:128,128*i:128*i+128]
    kaug[:,0:128]=k_ref[...]
    row=lax.broadcasted_iota(jnp.int32,(L,128),0)//128
    col=lax.broadcasted_iota(jnp.int32,(L,128),1)//2
    far=jnp.where(row<col-1,far_ref[0:1,:],jnp.where(row>col+1,far_ref[1:2,:],0.0))
    kaug[:,128:256]=(mask_ref[...]+far).astype(bf)
    vaug[:,0:128]=v_ref[...]
    for a in range(2):
        wb=jnp.broadcast_to(w_ref[a:a+1,:],(384,512))
        bn[:,128*a:128*a+128]=pltpu.roll(wb,0,1,stride=1,stride_axis=0)[:,0:128]
    def scores(i,slot):
        ri=rhs[:,256*i:256*i+256]
        lo,hi=max(0,i-1)*128,min(NT,i+2)*128
        off=(lo//128-(i-1))*128
        x=dot(kaug[...],ri)
        xn=x[lo:hi]+bn[off:off+hi-lo,:]
        ms=[jnp.max(xn,axis=0,keepdims=True)]
        s_ref[slot,lo:hi,:]=xn
        if lo>0:
            s_ref[slot,0:lo,:]=x[0:lo]; ms.append(jnp.max(x[0:lo],axis=0,keepdims=True))
        if hi<L:
            s_ref[slot,hi:L,:]=x[hi:L]; ms.append(jnp.max(x[hi:L],axis=0,keepdims=True))
        m=ms[0]
        for y in ms[1:]: m=jnp.maximum(m,y)
        return m
    lane=lax.broadcasted_iota(jnp.int32,(128,128),1)<64
    def finish(i,slot,m):
        e=jnp.exp(s_ref[slot]-m).astype(bf)
        e_ref[:,pl.ds(i*256,256)]=e
        o=dot_tl(e,vaug[...])
        num=jnp.where(lane,o[0:128,0:128],o[128:256,0:128])
        den=jnp.where(lane,o[0:128,128:256],o[128:256,128:256])
        r=1.0/den
        rows=pl.ds(i*128,128)
        o_ref[rows,:]=(num*r).astype(bf)
        r_ref[rows,:]=r
    m=scores(0,0)
    for i in range(NT):
        mn=scores(i+1,(i+1)%2) if i+1<NT else None
        finish(i,i%2,m)
        m=mn

def attn_fwd(q,k,v,mask,far,w):
    rows=q.shape[0]//L
    spec=pl.BlockSpec((L,128),lambda r,p:(r,p))
    return pl.pallas_call(fwd_kernel,
        grid=(rows,8),
        in_specs=[spec,spec,spec,
            pl.BlockSpec((None,L,128),lambda r,p:(r,0,0)),
            pl.BlockSpec((None,8,128),lambda r,p:(p,0,0)),
            pl.BlockSpec((None,8,512),lambda r,p:(p,0,0))],
        out_specs=[spec,pl.BlockSpec((None,None,L,NT*256),lambda r,p:(r,p,0,0)),spec],
        out_shape=[jax.ShapeDtypeStruct(q.shape,bf),jax.ShapeDtypeStruct((rows,8,L,NT*256),bf),jax.ShapeDtypeStruct(q.shape,f32)],
        scratch_shapes=[pltpu.VMEM((256,NT*256),bf),pltpu.VMEM((L,256),bf),pltpu.VMEM((L,256),bf),pltpu.VMEM((384,256),f32),pltpu.VMEM((2,L,256),f32)],
        compiler_params=pltpu.CompilerParams(vmem_limit_bytes=56*2**20),
        name="attn_fwd",
    )(q,k,v,mask,far,w)

THR=(12,16,23,32,46,64,91)
def bucket_np(d):
    n=np.abs(d); c=np.full_like(n,8)
    for t in THR: c=c+(n>=t)
    return np.where(n<8,n,c)+16*(d>0)
def tables(table):
    t=table.reshape(16,32).astype(f32)
    y=np.arange(512); y=np.where(y>=128,y-512,y)
    d=-128-y
    oh=(np.arange(32)[:,None]==bucket_np(d)[None,:]).astype(np.float32)
    w=jnp.dot(t,jnp.asarray(oh),precision=lax.Precision.HIGHEST)
    w=jnp.pad(w.reshape(8,2,512),((0,0),(0,6),(0,0)))
    lo=jnp.tile(t[:,15].reshape(8,1,2),(1,1,64)); hi=jnp.tile(t[:,31].reshape(8,1,2),(1,1,64))
    far=jnp.pad(jnp.concatenate([lo,hi],1),((0,0),(0,6),(0,0)))
    return far,w
def mask_cols(row_kind,text_length):
    pos=np.arange(L)
    kind=row_kind[:,None]
    seg=kind*(pos//384)[None]
    off=pos[None]-seg*384
    img=jnp.where(kind==1,256,1024)
    tl=jnp.where(seg==0,text_length[:,0:1],jnp.where(seg==1,text_length[:,1:2],text_length[:,2:3]))
    live=off<img+tl
    qseg=kind*np.minimum(np.arange(128)//2//3,2)[None]
    ok=live[:,:,None]&(seg[:,:,None]==qseg[:,None,:])
    return jnp.where(ok,0.0,NEG).astype(f32)

def bwd_kernel(q_ref,k_ref,v_ref,do_ref,o_ref,r_ref,e_ref,dq_ref,dk_ref,dv_ref,near_ref,far_ref,rhs,vaug,dobd,qaug,ds_ref,nacc):
    @pl.when((pl.program_id(0)==0)&(pl.program_id(1)==0))
    def _():
        rhs[...]=jnp.zeros_like(rhs)
        c=lax.broadcasted_iota(jnp.int32,(L,128),1)
        vaug[:,128:256]=(c<3).astype(f32).astype(bf)
        row=lax.broadcasted_iota(jnp.int32,(NT*256,128),0)
        col=lax.broadcasted_iota(jnp.int32,(NT*256,128),1)
        qaug[:,128:256]=(row//128==col).astype(f32).astype(bf)
    q=q_ref[...]; k=k_ref[...]
    vaug[:,0:128]=v_ref[...]
    dof=do_ref[...].astype(f32)*r_ref[...]
    dos=dof.astype(bf)
    dT=dos.T
    pT=(dos.astype(f32)*o_ref[...].astype(f32)).T
    D=jnp.concatenate([jnp.sum(pT[0:64],axis=0,keepdims=True),jnp.sum(pT[64:128],axis=0,keepdims=True)],0)
    D=-D
    D1=D.astype(bf); D2=(D-D1.astype(f32)); D3=(D2-D2.astype(bf).astype(f32)).astype(bf); D2=D2.astype(bf)
    lane=lax.broadcasted_iota(jnp.int32,(128,128),1)<64
    zero=jnp.zeros((128,128),bf)
    z13=jnp.zeros((13,128),bf)
    for i in range(NT):
        t=slice(128*i,128*i+128)
        for a in range(2):
            h=slice(64*a,64*a+64)
            c=slice(256*i+128*a,256*i+128*a+128)
            rhs[h,c]=dT[h,t]
            rhs[128:144,c]=jnp.concatenate([D1[a:a+1,t],D2[a:a+1,t],D3[a:a+1,t],z13],0)
            dobd[c,:]=jnp.where(lane==(a==0),dos[t],zero)
            qaug[c,0:128]=jnp.where(lane==(a==0),q[t],zero)
    nacc[...]=jnp.zeros_like(nacc)
    for i in range(NT):
        c=slice(256*i,256*i+256)
        lo,hi=max(0,i-1)*128,min(NT,i+2)*128
        off=(lo//128-(i-1))*128
        dp=dot(vaug[...],rhs[:,c])
        ds=e_ref[:,c].astype(f32)*dp
        nacc[off:off+hi-lo,:]+=ds[lo:hi]
        dsb=ds.astype(bf)
        ds_ref[:,c]=dsb
        g=dot_tl(dsb,k)
        dq_ref[128*i:128*i+128,:]=jnp.where(lane,g[0:128],g[128:256]).astype(bf)
    dv_ref[...]=dot(e_ref[...],dobd[...]).astype(bf)
    g=dot(ds_ref[...],qaug[...])
    dk_ref[...]=g[:,0:128].astype(bf)
    G=g[:,128:256]
    row=lax.broadcasted_iota(jnp.int32,(L,128),0)//128
    col=lax.broadcasted_iota(jnp.int32,(L,128),1)//2
    far_ref[0:1,:]=jnp.sum(jnp.where(row<col-1,G,0.0),axis=0,keepdims=True)
    far_ref[1:2,:]=jnp.sum(jnp.where(row>col+1,G,0.0),axis=0,keepdims=True)
    far_ref[2:8,:]=jnp.zeros((6,128),f32)
    near_ref[2:8,:]=jnp.zeros((6,512),f32)
    rev=(lax.broadcasted_iota(jnp.int32,(128,128),0)+lax.broadcasted_iota(jnp.int32,(128,128),1)==127).astype(f32)
    for a in range(2):
        x=jnp.dot(nacc[:,128*a:128*a+128],rev,precision=lax.Precision.HIGHEST,preferred_element_type=f32)
        x=jnp.concatenate([x,jnp.zeros((384,384),f32)],1)
        x=pltpu.roll(x,0,1,stride=1,stride_axis=0)
        near_ref[a:a+1,:]=jnp.sum(x,axis=0,keepdims=True)
def attn_bwd(q,k,v,do,o,r,e):
    rows=q.shape[0]//L
    spec=pl.BlockSpec((L,128),lambda r,p:(r,p))
    sds=jax.ShapeDtypeStruct
    return pl.pallas_call(bwd_kernel,
        grid=(rows,8),
        in_specs=[spec]*6+[pl.BlockSpec((None,None,L,NT*256),lambda r,p:(r,p,0,0))],
        out_specs=[spec]*3+[pl.BlockSpec((None,None,8,512),lambda r,p:(r,p,0,0)),pl.BlockSpec((None,None,8,128),lambda r,p:(r,p,0,0))],
        out_shape=[sds(q.shape,bf)]*3+[sds((rows,8,8,512),f32),sds((rows,8,8,128),f32)],
        scratch_shapes=[pltpu.VMEM((256,NT*256),bf),pltpu.VMEM((L,256),bf),pltpu.VMEM((NT*256,128),bf),pltpu.VMEM((NT*256,256),bf),pltpu.VMEM((L,NT*256),bf),pltpu.VMEM((384,256),f32)],
        compiler_params=pltpu.CompilerParams(vmem_limit_bytes=58*2**20),
        name="attn_bwd",
    )(q,k,v,do,o,r,e)
def table_grad(near,far):
    y=np.arange(512)
    oh=(bucket_np(y-255)[:,None]==np.arange(32)[None,:]).astype(np.float32)
    n=jnp.sum(near[:,:,0:2],0).reshape(16,512)
    g=jnp.dot(n,jnp.asarray(oh),precision=lax.Precision.HIGHEST)
    f=jnp.sum(far[:,:,0:2],0).reshape(8,2,64,2).sum(2)
    lo=f[:,0].reshape(16,1); hi=f[:,1].reshape(16,1)
    g=g+lo*np.eye(32,dtype=np.float32)[15][None]+hi*np.eye(32,dtype=np.float32)[31][None]
    return g.reshape(512)

EPS = 1e-06
SHARD = ("dp", "narrow")

def rms_norm(inputs, gain):
    return inputs * lax.rsqrt(jnp.mean(inputs * inputs, axis=-1, keepdims=True) + EPS) * gain

def gated(gate_in, up_in):
    return jax.nn.gelu(gate_in, approximate=True) * up_in

def contract_rows(left, right):
    return lax.dot_general(left, right, (((0,), (0,)), ((), ())), preferred_element_type=f32)

def contract_cols(left, right):
    return lax.dot_general(left, right, (((1,), (1,)), ((), ())), preferred_element_type=f32)

def gather(x):
    return lax.all_gather(x, SHARD, axis=0, tiled=True)

def scatter(x):
    return lax.psum_scatter(x, SHARD, scatter_dimension=0, tiled=True)

def per_device(tokens, row_kind, text_length, gain_attn, position_bias_table, weight_query, weight_key, weight_value, weight_out, gain_ffn, weight_gate, weight_up, weight_down, cotangent):
    small = lax.all_gather(jnp.concatenate([gain_attn, gain_ffn, position_bias_table]), SHARD, axis=0, tiled=False)
    qkv_w = gather(jnp.concatenate([weight_query, weight_key, weight_value], 1))
    gu_w = gather(jnp.concatenate([weight_out, weight_gate, weight_up], 1))
    down_w = gather(weight_down)
    d = qkv_w.shape[0]
    ff = weight_gate.shape[1]
    n1 = gain_attn.shape[0]
    gain_one = small[:, :n1].reshape(d).astype(f32)
    gain_two = small[:, n1:2 * n1].reshape(d).astype(f32)
    table = small[:, 2 * n1:].reshape(-1)
    far, w = tables(table)
    mask = mask_cols(row_kind, text_length)
    inputs = tokens.astype(f32)
    normed = rms_norm(inputs, gain_one).astype(bf)
    q = dot(normed, qkv_w[:, :d]).astype(bf)
    k = dot(normed, qkv_w[:, d:2 * d]).astype(bf)
    v = dot(normed, qkv_w[:, 2 * d:]).astype(bf)
    context, e, r = attn_fwd(q, k, v, mask, far, w)
    out_w, gate_w, up_w = gu_w[:, :d], gu_w[:, d:d + ff], gu_w[:, d + ff:]
    residual = inputs + dot(context, out_w)
    normed_ffn = rms_norm(residual, gain_two).astype(bf)
    gate_pre = dot(normed_ffn, gate_w)
    up_pre = dot(normed_ffn, up_w)
    hidden = gated(gate_pre, up_pre).astype(bf)
    output = (residual + dot(hidden, down_w)).astype(bf)
    grad_output = cotangent.astype(f32)
    grad_down = contract_rows(hidden, cotangent).astype(bf)
    s_down = scatter(grad_down)
    grad_hidden = contract_cols(cotangent, down_w)
    _, gate_pull = jax.vjp(gated, gate_pre, up_pre)
    gg, gu = gate_pull(grad_hidden)
    gg = gg.astype(bf)
    gu = gu.astype(bf)
    grad_normed_ffn = contract_cols(gg, gate_w) + contract_cols(gu, up_w)
    gw_gate = contract_rows(normed_ffn, gg).astype(bf)
    gw_up = contract_rows(normed_ffn, gu).astype(bf)
    _, norm_pull = jax.vjp(rms_norm, residual, gain_two)
    part, g_gain_two = norm_pull(grad_normed_ffn)
    grad_residual = grad_output + part
    gr_low = grad_residual.astype(bf)
    grad_out_w = contract_rows(context, gr_low).astype(bf)
    s_gu = scatter(jnp.concatenate([grad_out_w, gw_gate, gw_up], 1))
    grad_context = contract_cols(gr_low, out_w).astype(bf)
    gq, gk, gv, near, farsum = attn_bwd(q, k, v, grad_context, context, r, e)
    g_table = table_grad(near, farsum)
    gqkv = jnp.concatenate([contract_rows(normed, x).astype(bf) for x in (gq, gk, gv)], 1)
    s_qkv = scatter(gqkv)
    grad_normed = contract_cols(gq, qkv_w[:, :d]) + contract_cols(gk, qkv_w[:, d:2 * d]) + contract_cols(gv, qkv_w[:, 2 * d:])
    _, first_pull = jax.vjp(rms_norm, inputs, gain_one)
    share, g_gain_one = first_pull(grad_normed)
    grad_tokens = grad_residual + share
    small_g = jnp.concatenate([g_gain_one, g_gain_two, g_table])
    small_g = lax.psum(small_g, ("batch", "dp", "narrow"))
    at = lax.axis_index("dp") * lax.axis_size("narrow") + lax.axis_index("narrow")
    n2 = position_bias_table.shape[0]
    r_gain_one = lax.dynamic_slice_in_dim(small_g, at * n1, n1)
    r_gain_two = lax.dynamic_slice_in_dim(small_g, d + at * n1, n1)
    r_table = lax.dynamic_slice_in_dim(small_g, 2 * d + at * n2, n2)
    ar = lambda x: lax.psum(x, "batch").astype(f32)
    s_gu, s_down, s_qkv = ar(s_gu), ar(s_down), ar(s_qkv)
    return (output, grad_tokens, r_gain_one, r_table, s_qkv[:, :d], s_qkv[:, d:2 * d], s_qkv[:, 2 * d:], s_gu[:, :d], r_gain_two, s_gu[:, d:d + ff], s_gu[:, d + ff:], s_down)

def solution(mesh):
    placed = (
        P(("batch", "dp", "narrow"), None),
        P(("batch", "dp", "narrow")),
        P(("batch", "dp", "narrow"), None),
        P(("dp", "narrow")),
        P(("dp", "narrow")),
        P(("dp", "narrow"), None),
        P(("dp", "narrow"), None),
        P(("dp", "narrow"), None),
        P(("dp", "narrow"), None),
        P(("dp", "narrow")),
        P(("dp", "narrow"), None),
        P(("dp", "narrow"), None),
        P(("dp", "narrow"), None),
        P(("batch", "dp", "narrow"), None),
    )
    return jax.shard_map(
        per_device,
        mesh=mesh,
        in_specs=placed,
        out_specs=(
            P(("batch", "dp", "narrow"), None),
            P(("batch", "dp", "narrow"), None),
            P(("dp", "narrow")),
            P(("dp", "narrow")),
            P(("dp", "narrow"), None),
            P(("dp", "narrow"), None),
            P(("dp", "narrow"), None),
            P(("dp", "narrow"), None),
            P(("dp", "narrow")),
            P(("dp", "narrow"), None),
            P(("dp", "narrow"), None),
            P(("dp", "narrow"), None),
        ),
        check_vma=False,
    )
```

time: 1470 us -> 739 us (0.50)
  matrix products: 656 us -> 190 us
  waiting for transfers between devices: 411 us -> 268 us
  other arithmetic: 148 us -> 43.3 us
  Pallas kernels: 0 us -> 104 us
  local copies, waits for them, and re-layouts: 124 us -> 48.4 us
  loops' own time: 28.1 us -> 0 us
    dot_general x87 -> x9, matrix products: 519 us -> 72 us  [the longest x7 71.6 us: dot(): return jnp.dot(a, b, preferred_element_type=f32)]
    reduce_scatter x7 -> x2, waiting for transfers between devices: 352 us -> 145 us  [scatter(): return lax.psum_scatter(x, SHARD, scatter_dimension=0, tiled=True)]
    pallas_call x0 -> x2, Pallas kernels: none -> 104 us  [the longest x1 61.3 us: attn_bwd(): pl.pallas_call(bwd_kernel, grid=(rows, 8), in_specs=[spec] * 6 + [pl.Bloc...]
    convert_element_type x28 -> x3, other arithmetic: 81 us -> 1.72 us  [the longest x1 1.26 us: per_device(): ar = lambda x: lax.psum(x, 'batch').astype(f32)]
    all_gather x7 -> x3, waiting for transfers between devices: 1.66 us -> 66.3 us  [gather(): return lax.all_gather(x, SHARD, axis=0, tiled=True)]
    psum x1, blocking collectives: 11.8 us -> 43.4 us  [per_device(): small_g = lax.psum(small_g, ('batch', 'dp', 'narrow'))]
    another operation x2 -> x0, loops' own time: 28.1 us -> none  [the longest x1 21.9 us: one_row(): lax.scan(one_group, jnp.float32(0.0), jnp.arange(groups, dtype=jnp.int32))]
    concatenate x8 -> x7, other arithmetic: 1.44 us -> 29 us  [the longest x1 13.4 us: per_device(): jnp.concatenate([contract_rows(normed, x).astype(bf) for x in (gq, gk, gv...]
  transfers between devices with their start and end apart: 15 -> 7, of which waited for: 7 -> 6; matrix products, arithmetic and copies ran while one was open for 58% -> 21% of each run, Pallas kernels for 0% -> 6%
where the time goes in v1:
time: 739 us; the launch traced here: 730 us
  waiting for transfers between devices  268 us (36%)
  matrix products  190 us (26%)
  Pallas kernels  104 us (14%)
  blocking collectives  59.2 us (8%)
  local copies, waits for them, and re-layouts  48.4 us (7%)
  other arithmetic  43.3 us (6%)
  between operations  16.3 us (2%)
    reduce_scatter x2, waiting for transfers between devices, scatter(): return lax.psum_scatter(x, SHARD, scatter_dimension=0, tiled=True)  145 us
    dot_general x7, matrix products, dot(): return jnp.dot(a, b, preferred_element_type=f32)  71.6 us
    all_gather x3, waiting for transfers between devices, gather(): return lax.all_gather(x, SHARD, axis=0, tiled=True)  66.3 us
    dot_general x7, matrix products, contract_cols(): lax.dot_general(left, right, (((1,), (1,)), ((), ())), preferred_element_...  63 us
    pallas_call x1, Pallas kernels, attn_bwd(): pl.pallas_call(bwd_kernel, grid=(rows, 8), in_specs=[spec] * 6 + [pl.Bloc...  61.3 us
    dot_general x7, matrix products, contract_rows(): lax.dot_general(left, right, (((0,), (0,)), ((), ())), preferred_element_...  55.2 us
    psum x1, waiting for transfers between devices, per_device(): ar = lambda x: lax.psum(x, 'batch').astype(f32)  55.1 us
    psum x1, blocking collectives, per_device(): small_g = lax.psum(small_g, ('batch', 'dp', 'narrow'))  43.4 us
  transfers between devices with their start and end apart: 7, of which 6 were waited for; matrix products, arithmetic and copies ran while one was open for 21% of the time, Pallas kernels for 6%

profile of v1, /device:TPU:0, one launch (start us, length us, event | category | flops | bytes accessed | tf_op | source)
XLA Modules:
  0.0 730.0 jit_solution(12944966749022269390)
XLA Ops:
  7.2 0.7 all-gather.9.cloned.1.call-update
  8.0 2.0 pad_maximum_fusion.3
  10.1 2.7 pad_maximum_fusion.2
  13.0 3.0 copy.69
  16.0 0.6 dynamic-slice
  17.6 15.8 %all-reduce.2 = bf16[2560]{0:T(1024)(128)(2,1)S(1)} all-reduce(bf16[2560]{0:T(1024)(128)(2,1)S(1)} %dynamic-update-slice), channel_id=2, replica_groups=mesh['batch'=4,'dp'=4,'narrow'=2] {'dp','narrow'}, use_global_device_ids=true, to_apply=%add.2 | all-reduce | flops 2560 | bytes 10240
  35.2 4.3 copy.77
  39.5 0.7 pad.9.w_ref
  40.2 0.6 fusion.58
  40.8 0.6 select_maximum_fusion.far_ref
  41.4 2.0 compare_reduce_fusion
  43.5 0.5 fusion.21
  44.0 0.6 copy-done.9
  44.6 1.5 and_select_fusion.mask_ref
  46.1 10.1 %all-gather.9.cloned.1.call-done = bf16[2816,1024]{1,0:T(8,128)(2,1)} async-done(((bf16[352,1024]{1,0:T(8,128)(2,1)}), bf16[2816,1024]{1,0:T(8,128)(2,1)}) %all-gather.9.cloned.1.call-update) | async-done | bytes 5767184 | tf_op jit(solution)/shard_map/all_gather | solution.py:208
  56.2 12.8 %fusion.59 = f32[1152,2816]{1,0:T(8,128)} fusion(bf16[1152,1024]{1,0:T(8,128)(2,1)} %param.34, bf16[2816,1024]{1,0:T(8,128)(2,1)} %all-gather.9.cloned.1.call-done), kind=kOutput, calls=%fused_computation.105 | convolution fusion | flops 6643777536 | bytes 21102592 | tf_op jit(solution)/shard_map/dot_general | solution.py:205
  69.0 35.2 %all-gather.5.cloned.1.call-done = bf16[1024,3072]{1,0:T(8,128)(2,1)} async-done(((bf16[128,3072]{1,0:T(8,128)(2,1)}), bf16[1024,3072]{1,0:T(8,128)(2,1)}) %all-gather.5.cloned.1.call-update) | async-done | bytes 6291472 | tf_op jit(solution)/shard_map/all_gather | solution.py:208
  104.2 6.0 convolution_convert_fusion.4.v_ref
  110.2 4.2 convolution_convert_fusion.5.k_ref
  114.5 4.1 convolution_convert_fusion.6.q_ref
  118.6 43.1 %attn_fwd.1 = (bf16[1152,1024]{1,0:T(8,128)(2,1)}, bf16[1,8,1152,2304]{3,2,1,0:T(8,128)(2,1)}, f32[1152,1024]{1,0:T(8,128)}) custom-call(bf16[1152,1024]{1,0:T(8,128)(2,1)} %convolution_convert_fusion.6.q_ref, bf16[1152,1024]{1,0:T(8,128)(2,1)} %convolution_convert_fusion.5.k_ref, bf16[1152,1024]{1,0:T(8,128)(2,1)} %convolution_convert_fusion.4.v_ref, ...), custom_call_target="tpu_custom_call" | custom-call | tf_op jit(solution)/shard_map/attn_fwd/pallas_call | solution.py:71
  161.7 21.0 %all-gather.7.cloned.1.call-done = bf16[1024,6656]{1,0:T(8,128)(2,1)} async-done(((bf16[128,6656]{1,0:T(8,128)(2,1)}), bf16[1024,6656]{1,0:T(8,128)(2,1)}) %all-gather.7.cloned.1.call-update) | async-done | bytes 13631504 | tf_op jit(solution)/shard_map/all_gather | solution.py:208
  182.7 5.6 multiply_reduce_fusion.2
  188.8 1.7 copy-done.5
  190.5 12.3 %fusion.11 = f32[1152,2816]{1,0:T(8,128)} fusion(bf16[1152,1024]{0,1:T(8,128)(2,1)S(1)} %multiply_convert_fusion.2, bf16[1024,6656]{1,0:T(8,128)(2,1)} %all-gather.7.cloned.1.call-done), kind=kOutput, calls=%fused_computation.28 | convolution fusion | flops 6643777536 | bytes 21102592 | tf_op jit(solution)/shard_map/dot_general | solution.py:12
  202.8 27.1 %fusion.6 = (bf16[1152,2816]{1,0:T(8,128)(2,1)}, bf16[1152,2816]{1,0:T(8,128)(2,1)}, bf16[1152,2816]{1,0:T(8,128)(2,1)}) fusion(f32[1152,2816]{1,0:T(8,128)} %fusion.59, f32[1152,2816]{1,0:T(8,128)} %fusion.11, bf16[1152,1024]{0,1:T(8,128)(2,1)} %copy-done.5, bf16[1024,6656]{1,0:T(8,128)(2,1)} %all-gather.7.cloned.1.call-done), kind=kOutput, calls=%fused_computation.9 | convolution fusion | flops 6728122368 | bytes 53542912 | tf_op jit(solution)/shard_map/dot_general | solution.py:12
  229.8 11.6 %fusion.9 = f32[1152,1024]{0,1:T(8,128)S(1)} fusion(bf16[1152,2816]{1,0:T(8,128)(2,1)} %get-tuple-element.74, bf16[1024,6656]{1,0:T(8,128)(2,1)} %all-gather.7.cloned.1.call-done), kind=kOutput, calls=%fused_computation.26 | convolution fusion | flops 6643777536 | bytes 16973824 | tf_op jit(solution)/shard_map/dot_general | solution.py:205
  241.4 13.5 %multiply_reduce_fusion = (f32[1024]{0:T(1024)}, f32[1152]{0:T(1024)S(1)}, f32[1152,1024]{0,1:T(8,128)S(1)}) fusion(f32[1152,1024]{0,1:T(8,128)S(1)} %get-tuple-element.93, f32[1152]{0:T(1024)S(1)} %fusion.40, f32[1024]{0:T(1024)S(1)} %get-tuple-element.83, f32[1152,1024]{0,1:T(8,128)S(1)} %fusion.9, bf16[1152,2816]{1,0:T(8,128)(2,1)} %get-tuple-element.73, ...), kind=kOutput, calls=%fused_computation.40 | convolution fusion | flops 6652033024 | bytes 26428416 | tf_op jit(solution)/shard_map/dot_general | solution.py:205
  255.0 1.3 fusion.19
  256.2 7.3 convolution_convert_fusion.3.do_ref
  263.5 61.3 %attn_bwd.1 = (bf16[1152,1024]{1,0:T(8,128)(2,1)}, bf16[1152,1024]{1,0:T(8,128)(2,1)}, bf16[1152,1024]{1,0:T(8,128)(2,1)}, f32[1,8,8,512]{3,2,1,0:T(8,128)}, f32[1,8,8,128]{3,2,1,0:T(8,128)}) custom-call(bf16[1152,1024]{1,0:T(8,128)(2,1)} %convolution_convert_fusion.6.q_ref, bf16[1152,1024]{1,0:T(8,128)(2,1)} %convolution_convert_fusion.5.k_ref, ...), custom_call_target="tpu_custom_call" | custom-call | tf_op jit(solution)/shard_map/attn_bwd/pallas_call | solution.py:173
  324.8 5.6 convolution_convert_fusion.10
  330.5 3.5 convolution_convert_fusion.8
  333.9 3.5 convolution_convert_fusion.9
  337.4 13.4 %pad_maximum_fusion.1 = bf16[1024,3072]{0,1:T(8,128)(2,1)} fusion(bf16[1024,1024]{0,1:T(8,128)(2,1)S(1)} %convolution_convert_fusion.8, bf16[1024,1024]{0,1:T(8,128)(2,1)S(1)} %convolution_convert_fusion.9, bf16[1024,1024]{0,1:T(8,128)(2,1)S(1)} %convolution_convert_fusion.10), kind=kLoop, calls=%fused_computation.20 | loop fusion | flops 18874368 | bytes 12582912 | tf_op jit(solution)/shard_map/concatenate | solution.py:259
  350.8 8.7 %copy.98 = bf16[1024,3072]{1,0:T(8,128)(2,1)} copy(bf16[1024,3072]{0,1:T(8,128)(2,1)} %pad_maximum_fusion.1) | data formatting | bytes 12582912
  359.5 12.7 %convolution_convert_fusion = bf16[2816,1024]{1,0:T(8,128)(2,1)} fusion(bf16[1152,2816]{1,0:T(8,128)(2,1)} %get-tuple-element.75, bf16[1152,1024]{1,0:T(8,128)(2,1)} %param.34), kind=kOutput, calls=%fused_computation.21 | convolution fusion | flops 6646661120 | bytes 14614528 | tf_op jit(solution)/shard_map/dot_general | solution.py:202
  372.3 7.8 %convolution_convert_fusion.7 = bf16[1024,1024]{0,1:T(8,128)(2,1)} fusion(bf16[1152,1024]{1,0:T(8,128)(2,1)} %get-tuple-element.20.o_ref, f32[1152,1024]{0,1:T(8,128)} %copy-done.1), kind=kOutput, calls=%fused_computation.51 | convolution fusion | flops 2418147328 | bytes 9175040 | tf_op jit(solution)/shard_map/dot_general | solution.py:202
  380.1 4.1 copy.86
  384.2 11.2 %convolution_convert_fusion.2 = bf16[1024,2816]{1,0:T(8,128)(2,1)S(1)} fusion(bf16[1152,1024]{0,1:T(8,128)(2,1)} %copy-done.5, bf16[1152,2816]{1,0:T(8,128)(2,1)} %get-tuple-element.73), kind=kOutput, calls=%fused_computation.23 | convolution fusion | flops 6646661120 | bytes 14614528 | tf_op jit(solution)/shard_map/dot_general | solution.py:202
  395.4 11.0 %convolution_convert_fusion.1 = bf16[1024,2816]{1,0:T(8,128)(2,1)S(1)} fusion(bf16[1152,1024]{0,1:T(8,128)(2,1)S(1)} %copy-done.6, bf16[1152,2816]{1,0:T(8,128)(2,1)} %get-tuple-element.74), kind=kOutput, calls=%fused_computation.22 | convolution fusion | flops 6646661120 | bytes 14614528 | tf_op jit(solution)/shard_map/dot_general | solution.py:202
  406.4 10.2 %pad_maximum_fusion = bf16[1024,6656]{1,0:T(8,128)(2,1)} fusion(bf16[1024,2816]{1,0:T(8,128)(2,1)S(1)} %convolution_convert_fusion.1, bf16[1024,2816]{1,0:T(8,128)(2,1)S(1)} %convolution_convert_fusion.2, bf16[1024,1024]{1,0:T(8,128)(2,1)S(1)} %copy-done.3), kind=kLoop, calls=%fused_computation.2 | loop fusion | flops 40894464 | bytes 27262976 | tf_op jit(solution)/shard_map/concatenate | solution.py:255
  417.0 0.8 slice.90
  418.3 0.9 slice.89
  419.6 5.4 fusion.30
  425.1 4.7 fusion.33
  429.7 7.8 %fusion.18 = (f32[1024]{0:T(1024)S(1)}, f32[1152]{0:T(1024)S(1)}, f32[1152,1024]{0,1:T(8,128)}) fusion(bf16[1152,1024]{0,1:T(8,128)(2,1)S(1)} %copy.69, f32[1152]{0:T(1024)S(1)} %fusion.39, f32[1024]{0:T(1024)S(1)} %get-tuple-element.84, bf16[1152,1024]{1,0:T(8,128)(2,1)S(1)} %copy-done.23, bf16[1024,3072]{1,0:T(8,128)(2,1)} %all-gather.5.cloned.1.call-done, ...), kind=kOutput, calls=%fused_computation.35 | convolution fusion | flops 2426533888 | bytes 20988928 | tf_op jit(solution)/shard_map/dot_general | solution.py:205
  437.6 2.4 copy.99
  440.0 44.1 %reduce-scatter.8.cloned.1.call-done = bf16[352,1024]{1,0:T(8,128)(2,1)} async-done(((bf16[2816,1024]{1,0:T(8,128)(2,1)}), bf16[352,1024]{1,0:T(8,128)(2,1)}) %reduce-scatter.8.cloned.1.call-update) | async-done | bytes 720912 | tf_op jit(solution)/shard_map/reduce_scatter | solution.py:211
  484.1 101.4 %reduce-scatter.6.cloned.1.call-done = bf16[128,6656]{1,0:T(8,128)(2,1)} async-done(((bf16[1024,6656]{1,0:T(8,128)(2,1)}), bf16[128,6656]{1,0:T(8,128)(2,1)}) %reduce-scatter.6.cloned.1.call-update) | async-done | bytes 1703952 | tf_op jit(solution)/shard_map/reduce_scatter | solution.py:211
  585.5 7.1 fusion.20
  592.6 6.4 copy.88
  599.0 12.4 %add_convert_fusion = bf16[1152,1024]{0,1:T(8,128)(2,1)S(1)} fusion(f32[1152,1024]{0,1:T(8,128)} %copy-done, bf16[1152,2816]{1,0:T(8,128)(2,1)} %get-tuple-element.75, bf16[2816,1024]{1,0:T(8,128)(2,1)} %all-gather.9.cloned.1.call-done), kind=kOutput, calls=%fused_computation.43 | convolution fusion | flops 6646136832 | bytes 19333120 | tf_op jit(solution)/shard_map/dot_general | solution.py:12
  611.4 2.5 copy.87
  613.9 43.4 %psum.28 = f32[2560]{0:T(1024)S(1)} all-reduce(f32[2560]{0:T(1024)S(1)} %pad_maximum_fusion.4), channel_id=1, replica_groups=mesh['batch'=4,'dp'=4,'narrow'=2] {'batch','dp','narrow'}, use_global_device_ids=true, to_apply=%region_7.8 | all-reduce | flops 2560 | bytes 20480 | tf_op jit(solution)/shard_map/psum | solution.py:266
  657.3 0.6 dynamic_slice.10
  657.8 0.6 fusion.55
  658.4 55.1 %all-reduce.6.cloned.1.call-done = (bf16[128,3072]{0,1:T(8,128)(2,1)}, bf16[128,6656]{1,0:T(8,128)(2,1)}, bf16[352,1024]{1,0:T(8,128)(2,1)}) async-done(((bf16[128,3072]{0,1:T(8,128)(2,1)}, bf16[128,6656]{1,0:T(8,128)(2,1)}, bf16[352,1024]{1,0:T(8,128)(2,1)}), (bf16[128,3072]{0,1:T(8,128)(2,1)}, bf16[128,6656]{1,0:T(8,128)(2,1)}, bf16[352,1024]{1,0:T(8,128)(2,1)})) %all-reduce.6.cloned.1.call-update) | async-done | bytes 3211280 | tf_op jit(solution)/shard_map/psum | solution.py:272
  713.5 3.2 fusion.53
  716.7 1.9 slice.115
  718.7 1.0 copy.89
  719.7 1.0 copy.90
  720.7 1.0 copy.91
  721.7 1.3 convert_element_type.127
  (106 shorter events, 3.7 us)
Async XLA Ops:
  7.2 49.0 %all-gather.9.cloned.1.call-start = ((), (), s32[]{:S(2)}) async-start(), calls=%async_computation.5 | async-start | bytes 6488064 | tf_op jit(solution)/shard_map/all_gather | solution.py:208
  7.9 96.3 %all-gather.5.cloned.1.call-start = ((), (), s32[]{:S(2)}) async-start(), calls=%async_computation.3 | async-start | bytes 7077888 | tf_op jit(solution)/shard_map/all_gather | solution.py:208
  10.0 6.0 copy-start.27
  10.0 7.2 copy-start.18
  10.1 7.2 copy-start.19
  10.1 7.2 copy-start.20
  10.1 24.9 %copy-start.11 = (f32[32,512,1]{1,0,2:T(8,128)S(1)}, f32[32,512,1]{1,0,2:T(8,128)}, u32[]{:S(2)}) copy-start(f32[32,512,1]{1,0,2:T(8,128)} %constant.103) | copy-start | bytes 196612
  10.1 172.6 %all-gather.7.cloned.1.call-start = ((), (), s32[]{:S(2)}) async-start(), calls=%async_computation.4 | async-start | bytes 15335424 | tf_op jit(solution)/shard_map/all_gather | solution.py:208
  12.9 424.7 %reduce-scatter.10.cloned.1.call-start = ((), (), s32[]{:S(2)}) async-start(), calls=%async_computation.8 | async-start | bytes 7077888
  12.9 27.3 %copy-start.14 = (s32[1,3]{1,0:T(1,128)S(1)}, s32[1,3]{1,0:T(1,128)}, u32[]{:S(2)}) copy-start(s32[1,3]{1,0:T(1,128)} %param.23) | copy-start | bytes 40
  12.9 27.9 %copy-start.12 = (s32[1,1152]{1,0:T(1,128)S(1)}, s32[1,1152]{1,0:T(1,128)}, u32[]{:S(2)}) copy-start(s32[1,1152]{1,0:T(1,128)} %constant.83.clone) | copy-start | bytes 13828
  13.0 28.5 %copy-start.13 = (s32[1,1152]{1,0:T(1,128)S(1)}, s32[1,1152]{1,0:T(1,128)}, u32[]{:S(2)}) copy-start(s32[1,1152]{1,0:T(1,128)} %constant.84.clone) | copy-start | bytes 13828
  13.0 30.5 %copy-start.26 = (s32[1,128]{1,0:T(1,128)S(1)}, s32[1,128]{1,0:T(1,128)}, u32[]{:S(2)}) copy-start(s32[1,128]{1,0:T(1,128)} %constant.85.clone) | copy-start | bytes 1540
  44.0 0.6 copy-start.9
  104.2 6.0 copy-start.21
  188.3 66.6 %copy-start = (f32[1152,1024]{0,1:T(8,128)}, f32[1152,1024]{0,1:T(8,128)S(1)}, u32[]{:S(2)}) copy-start(f32[1152,1024]{0,1:T(8,128)S(1)} %get-tuple-element.93) | copy-start | bytes 14155780
  188.8 1.7 copy-start.5
  241.4 13.5 %copy-start.2 = (bf16[1152,1024]{0,1:T(8,128)(2,1)S(1)}, bf16[1152,1024]{0,1:T(8,128)(2,1)}, u32[]{:S(2)}) copy-start(bf16[1152,1024]{0,1:T(8,128)(2,1)} %copy.77) | copy-start | bytes 7077892
  256.2 7.3 copy-start.1
  324.8 5.7 copy-start.22
  330.5 3.5 copy-start.25
  359.5 124.7 %reduce-scatter.8.cloned.1.call-start = ((), (), s32[]{:S(2)}) async-start(), calls=%async_computation.7 | async-start | bytes 6488064 | tf_op jit(solution)/shard_map/reduce_scatter | solution.py:211
  372.2 213.3 %reduce-scatter.6.cloned.1.call-start = ((), (), s32[]{:S(2)}) async-start(), calls=%async_computation.6 | async-start | bytes 15335424 | tf_op jit(solution)/shard_map/reduce_scatter | solution.py:211
  384.2 11.2 %copy-start.6 = (bf16[1152,1024]{0,1:T(8,128)(2,1)S(1)}, bf16[1152,1024]{0,1:T(8,128)(2,1)}, u32[]{:S(2)}) copy-start(bf16[1152,1024]{0,1:T(8,128)(2,1)} %copy-done.5) | copy-start | bytes 7077892
  395.4 11.0 %copy-start.3 = (bf16[1024,1024]{1,0:T(8,128)(2,1)S(1)}, bf16[1024,1024]{1,0:T(8,128)(2,1)}, u32[]{:S(2)}) copy-start(bf16[1024,1024]{1,0:T(8,128)(2,1)} %copy.86) | copy-start | bytes 6291460
  416.7 2.6 copy-start.8
  416.7 2.6 copy-start.16
  416.7 2.6 copy-start.17
  416.7 296.8 %all-reduce.6.cloned.1.call-start = ((), (), s32[]{:S(2)}) async-start(), calls=%async_computation.9 | async-start | bytes 6422528 | tf_op jit(solution)/shard_map/psum | solution.py:272
  419.6 5.4 copy-start.24
  425.1 4.7 copy-start.23
  429.7 7.8 %copy-start.10 = (f32[1152]{0:T(1024)S(1)}, f32[1152]{0:T(1024)}, u32[]{:S(2)}) copy-start(f32[1152]{0:T(1024)} %copy-done.9) | copy-start | bytes 13828
  611.4 2.5 copy-start.15
  713.5 5.0 copy-start.4
  716.7 5.0 copy-start.7
Sparse Core Ops, SparseCore 0:
  9.9 46.2 all-gather.8
  58.7 45.5 all-gather.4
  106.1 76.5 all-gather.6
  359.6 61.7 reduce-scatter.9
  425.1 59.0 reduce-scatter.7
  487.5 97.9 reduce-scatter.5
  588.6 124.8 all-reduce.5

commit v2 on v1

--- a/solution.py
+++ b/solution.py
@@ -1,3 +1,5 @@
+import functools
+
 import jax
 import jax.numpy as jnp
 import numpy as np
@@ -6,6 +8,8 @@
 from jax.experimental.pallas import tpu as pltpu
 from jax.sharding import PartitionSpec as P
 
+EPS = 1e-06
+SHARD = ("dp", "narrow")
 bf=jnp.bfloat16; f32=jnp.float32
 T=128; L=1152; NT=L//T
 NEG=-1e30
@@ -189,91 +193,354 @@
     g=g+lo*np.eye(32,dtype=np.float32)[15][None]+hi*np.eye(32,dtype=np.float32)[31][None]
     return g.reshape(512)
 
-EPS = 1e-06
-SHARD = ("dp", "narrow")
+MESH = pl.DeviceIdType.MESH
+
+def places():
+    b, m, c = lax.axis_index("batch"), lax.axis_index("dp"), lax.axis_index("narrow")
+    x, y = lax.rem(m, 2), m // 2
+    mx = y * 2 + (1 - x)
+    my = (1 - y) * 2 + x
+    md = (1 - y) * 2 + (1 - x)
+    return b, m, c, mx, my, md
+
+def greet(devices):
+    barrier = pltpu.get_barrier_semaphore()
+    for d in devices:
+        pl.semaphore_signal(barrier, inc=1, device_id=d, device_id_type=MESH)
+    pl.semaphore_wait(barrier, len(devices))
+
+def qkv_kernel(x_ref, small_ref, wq_ref, wk_ref, wv_ref, q_ref, k_ref, v_ref, n_ref, w_out, W, acc, xh, send, recv, local):
+    b, m, c, mx, my, md = places()
+    o = 1 - c
+    nx, ny, nc = (b, mx, c), (b, my, c), (b, m, o)
+    d = wq_ref.shape[1]
+    rows = wq_ref.shape[0]
+    half = rows // 2
+    me = m * 2 + c
+    W[me, :, 0:d] = wq_ref[...]
+    W[me, :, d:2 * d] = wk_ref[...]
+    W[me, :, 2 * d:3 * d] = wv_ref[...]
+    W[me, :, 3 * d:3 * d + 128] = small_ref[...]
+    greet([nx, ny, nc])
+    def push(src, n, to):
+        return pltpu.make_async_remote_copy(src_ref=src, dst_ref=src, send_sem=send.at[n], recv_sem=recv.at[n], device_id=to, device_id_type=MESH)
+    top, low = pl.ds(0, half), pl.ds(half, half)
+    s0, s1, s2 = push(W.at[me], 0, nx), push(W.at[me], 1, ny), push(W.at[me], 2, nc)
+    s0.start(); s1.start(); s2.start()
+    x = x_ref[...].astype(f32)
+    xh[...] = x * lax.rsqrt(jnp.mean(x * x, axis=-1, keepdims=True) + EPS)
+    def chunk(j, first):
+        cols = pl.ds(pl.multiple_of(j * 2 * rows, 2 * rows), 2 * rows)
+        gain = jnp.concatenate([W[2 * j, 0:1, 3 * d:3 * d + rows], W[2 * j + 1, 0:1, 3 * d:3 * d + rows]], 1).astype(f32)
+        n = (xh[:, cols] * gain).astype(bf)
+        n_ref[:, cols] = n
+        for t in range(3):
+            w = W[pl.ds(2 * j, 2), :, t * d:t * d + d].reshape(2 * rows, d)
+            p = dot(n, w)
+            if first:
+                acc[:, t * d:t * d + d] = p
+            else:
+                acc[:, t * d:t * d + d] = acc[:, t * d:t * d + d] + p
+    ix, iy, idg = mx * 2 + c, my * 2 + c, md * 2 + c
+    jx, jy, jdg = mx * 2 + o, my * 2 + o, md * 2 + o
+    def here(ref, n):
+        return pltpu.make_async_remote_copy(src_ref=ref, dst_ref=ref, send_sem=send.at[n], recv_sem=recv.at[n], device_id=nc, device_id_type=MESH)
+    here(W.at[m * 2 + o], 2).wait_recv()
+    chunk(m, True)
+    here(W.at[ix], 0).wait_recv()
+    s3, s5 = push(W.at[ix, top], 3, ny), push(W.at[ix], 5, nc)
+    s3.start(); s5.start()
+    here(W.at[iy], 1).wait_recv()
+    s4, s6 = push(W.at[iy, low], 4, nx), push(W.at[iy], 6, nc)
+    s4.start(); s6.start()
+    here(W.at[jx], 5).wait_recv()
+    chunk(mx, False)
+    here(W.at[jy], 6).wait_recv()
+    chunk(my, False)
+    here(W.at[idg, top], 3).wait_recv()
+    here(W.at[idg, low], 4).wait_recv()
+    s7 = push(W.at[idg], 7, nc)
+    s7.start()
+    here(W.at[jdg], 7).wait_recv()
+    keep = pltpu.make_async_copy(W, w_out, local)
+    keep.start()
+    chunk(md, False)
+    q_ref[...] = acc[:, 0:d].astype(bf)
+    k_ref[...] = acc[:, d:2 * d].astype(bf)
+    v_ref[...] = acc[:, 2 * d:3 * d].astype(bf)
+    for s in (s0, s1, s2, s3, s4, s5, s6, s7):
+        s.wait_send()
+    keep.wait()
+
+def gather_qkv(tokens, small, wq, wk, wv):
+    L_, d = tokens.shape
+    rows = wq.shape[0]
+    sds = jax.ShapeDtypeStruct
+    vm = pl.BlockSpec(memory_space=pltpu.VMEM)
+    return pl.pallas_call(qkv_kernel,
+        in_specs=[vm] * 5,
+        out_specs=[vm] * 4 + [pl.BlockSpec(memory_space=pl.ANY)],
+        out_shape=[sds((L_, d), bf)] * 4 + [sds((8, rows, 3 * d + 128), bf)],
+        scratch_shapes=[pltpu.VMEM((8, rows, 3 * d + 128), bf), pltpu.VMEM((L_, 3 * d), f32), pltpu.VMEM((L_, d), f32),
+                        pltpu.SemaphoreType.DMA((8,)), pltpu.SemaphoreType.DMA((8,)), pltpu.SemaphoreType.DMA],
+        compiler_params=pltpu.CompilerParams(collective_id=1, has_side_effects=True, vmem_limit_bytes=60 * 2**20),
+        name="gather_qkv")(tokens, small, wq, wk, wv)
+
+def gather_steps(gu_in, dn_in, wo_in, gu, dn, wo, send, recv, local):
+    b, m, c, mx, my, md = places()
+    o = 1 - c
+    z = lax.rem(b, 2)
+    oz = 1 - z
+    nx, ny, nc, nz = (b, mx, c), (b, my, c), (b, m, o), (b + 1 - 2 * z, m, c)
+    me, it = m * 2 + c, m * 2 + o
+    ix, iy, idg = mx * 2 + c, my * 2 + c, md * 2 + c
+    jx, jy, jdg = mx * 2 + o, my * 2 + o, md * 2 + o
+    def copy(src, dst, n, to):
+        return pltpu.make_async_remote_copy(src_ref=src, dst_ref=dst, send_sem=send.at[n], recv_sem=recv.at[n], device_id=to, device_id_type=MESH)
+    def push(ref, n, to):
+        return copy(ref, ref, n, to)
+    def got(ref, n):
+        copy(ref, ref, n, nc).wait_recv()
+    def first(src, dst, n):
+        for t, to in enumerate((nx, ny, nc)):
+            copy(src, dst, n + t, to).start()
+    def halves(ref, i):
+        h = ref.shape[1] // 2
+        return ref.at[i, pl.ds(0, h)], ref.at[i, pl.ds(h, h)]
+    def second(ref, n, onward=None):
+        got(ref.at[ix], n)
+        push(halves(ref, ix)[0], n + 3, ny).start()
+        push(ref.at[ix], n + 5, nc).start()
+        if onward is not None:
+            push(ref.at[ix], onward, nz).start()
+        got(ref.at[iy], n + 1)
+        push(halves(ref, iy)[1], n + 4, nx).start()
+        push(ref.at[iy], n + 6, nc).start()
+        if onward is not None:
+            push(ref.at[iy], onward + 1, nz).start()
+    def third(ref, n, onward=None):
+        got(halves(ref, idg)[0], n + 3)
+        got(halves(ref, idg)[1], n + 4)
+        push(ref.at[idg], n + 7, nc).start()
+        if onward is not None:
+            push(ref.at[idg], onward + 2, nz).start()
+    def last(src, ref, n, onward=None):
+        for t, i in ((2, it), (5, jx), (6, jy), (7, jdg)):
+            got(ref.at[i], n + t)
+        for t in (0, 1, 2):
+            copy(src, ref.at[me], n + t, nc).wait_send()
+        push(halves(ref, ix)[0], n + 3, ny).wait_send()
+        push(halves(ref, iy)[1], n + 4, nx).wait_send()
+        for t, i in ((5, ix), (6, iy), (7, idg)):
+            push(ref.at[i], n + t, nc).wait_send()
+        if onward is not None:
+            for t, i in enumerate((ix, iy, idg)):
+                push(ref.at[i], onward + t, nz).wait_send()
+    mine, other = gu.at[z], gu.at[oz]
+    keeps = [pltpu.make_async_copy(gu_in, gu.at[:, me], local.at[0]), pltpu.make_async_copy(dn_in, dn.at[me], local.at[1]), pltpu.make_async_copy(wo_in, wo.at[me], local.at[2])]
+    def begin():
+        greet([nx, ny, nc, nz])
+        first(gu_in.at[z], mine.at[me], 0)
+        first(dn_in, dn.at[me], 8)
+        first(wo_in, wo.at[me], 16)
+        copy(gu_in.at[oz], other.at[me], 24, nc).start()
+        for k in keeps:
+            k.start()
+    def z_second(ts):
+        for t, i in ts:
+            got(other.at[i], 25 + t)
+            push(other.at[i], 28 + t, nc).start()
+    def end():
+        third(wo, 16)
+        z_second([(2, idg)])
+        last(gu_in.at[z], mine, 0, 25)
+        last(dn_in, dn, 8)
+        last(wo_in, wo, 16)
+        got(other.at[it], 24)
+        copy(gu_in.at[oz], other.at[me], 24, nc).wait_send()
+        for t, i, j in ((0, ix, jx), (1, iy, jy), (2, idg, jdg)):
+            got(other.at[j], 28 + t)
+            push(other.at[i], 28 + t, nc).wait_send()
+        for k in keeps:
+            k.wait()
+    def at5():
+        third(mine, 0, 25)
+        second(dn, 8)
+    def at7():
+        z_second([(0, ix), (1, iy)])
+        third(dn, 8)
+        second(wo, 16)
+    return {0: begin, 3: lambda: second(mine, 0, 25), 5: at5, 7: at7}, end
+
+def fwd_gather_kernel(*refs):
+    (q_ref, k_ref, v_ref, mask_ref, far_ref, w_ref, gu_in, dn_in, wo_in, o_ref, e_ref, r_ref, gu, dn, wo,
+     rhs, kaug, vaug, bn, s_ref, send, recv, local) = refs
+    before, end = gather_steps(gu_in, dn_in, wo_in, gu, dn, wo, send, recv, local)
+    p = pl.program_id(1)
+    for at, act in before.items():
+        pl.when(p == at)(act)
+    fwd_kernel(q_ref, k_ref, v_ref, mask_ref, far_ref, w_ref, o_ref, e_ref, r_ref, rhs, kaug, vaug, bn, s_ref)
+    pl.when(p == 7)(end)
+
+def attn_fwd_gather(q, k, v, mask, far, w, gu, dn, wo):
+    rows = q.shape[0] // L
+    spec = pl.BlockSpec((L, 128), lambda r, p: (r, p))
+    hbm = pl.BlockSpec(memory_space=pl.ANY)
+    sds = jax.ShapeDtypeStruct
+    return pl.pallas_call(fwd_gather_kernel,
+        grid=(rows, 8),
+        in_specs=[spec, spec, spec,
+            pl.BlockSpec((None, L, 128), lambda r, p: (r, 0, 0)),
+            pl.BlockSpec((None, 8, 128), lambda r, p: (p, 0, 0)),
+            pl.BlockSpec((None, 8, 512), lambda r, p: (p, 0, 0)), hbm, hbm, hbm],
+        out_specs=[spec, pl.BlockSpec((None, None, L, NT * 256), lambda r, p: (r, p, 0, 0)), spec, hbm, hbm, hbm],
+        out_shape=[sds(q.shape, bf), sds((rows, 8, L, NT * 256), bf), sds(q.shape, f32),
+                   sds((2, 8) + gu.shape[1:], bf), sds((8,) + dn.shape, bf), sds((8,) + wo.shape, bf)],
+        scratch_shapes=[pltpu.VMEM((256, NT * 256), bf), pltpu.VMEM((L, 256), bf), pltpu.VMEM((L, 256), bf), pltpu.VMEM((384, 256), f32), pltpu.VMEM((2, L, 256), f32),
+                        pltpu.SemaphoreType.DMA((31,)), pltpu.SemaphoreType.DMA((31,)), pltpu.SemaphoreType.DMA((3,))],
+        compiler_params=pltpu.CompilerParams(collective_id=2, has_side_effects=True, vmem_limit_bytes=56 * 2**20),
+        name="attn_fwd_gather")(q, k, v, mask, far, w, gu, dn, wo)
+
+GELU_C = float(np.sqrt(2.0 / np.pi))
+def dot_nt(a, b):
+    return lax.dot_general(a, b, (((1,), (1,)), ((), ())), preferred_element_type=f32)
+
+def ffn_kernel(x_ref, ctx_ref, g_ref, gain_ref, wo_ref, gu_ref, dn_ref,
+               out_ref, gres_ref, gctx_ref, dwo_ref, ggain_ref, dgu_ref, ddn_ref, res, n, acc):
+    j = pl.program_id(0)
+    steps = pl.num_programs(0)
+    R = x_ref.shape[0]
+    d = x_ref.shape[1]
+    CH = 384
+    @pl.when(j == 0)
+    def _():
+        for t in range(0, R, CH):
+            s = slice(t, t + CH)
+            y = x_ref[s, :].astype(f32) + dot(ctx_ref[s, :], wo_ref[...])
+            res[s, :] = y
+            acc[s, :] = y
+            n[s, :] = (y * lax.rsqrt(jnp.mean(y * y, axis=-1, keepdims=True) + EPS) * gain_ref[0:1, :]).astype(bf)
+        gres_ref[...] = jnp.zeros_like(gres_ref)
+    wg = gu_ref[0].reshape(d, gu_ref.shape[-1])
+    wu = gu_ref[1].reshape(d, gu_ref.shape[-1])
+    wd = dn_ref[...]
+    nn = n[...]
+    g = g_ref[...]
+    v = dot(nn, wg)
+    u = dot(nn, wu)
+    gh = dot_nt(g, wd)
+    v2 = v * v
+    th = jnp.tanh(GELU_C * v * (1.0 + 0.044715 * v2))
+    half = 0.5 * (1.0 + th)
+    gel = v * half
+    h = (gel * u).astype(bf)
+    dgel = half + 0.5 * v * (1.0 - th * th) * (GELU_C * (1.0 + 3 * 0.044715 * v2))
+    gg = (gh * u * dgel).astype(bf)
+    gu = (gh * gel).astype(bf)
+    acc[...] = acc[...] + dot(h, wd)
+    gres_ref[...] = gres_ref[...] + dot_nt(jnp.concatenate([gg, gu], 1), jnp.concatenate([wg, wu], 1))
+    dgu_ref[0] = dot_tl(nn, gg).astype(bf).reshape(dgu_ref.shape[1:])
+    dgu_ref[1] = dot_tl(nn, gu).astype(bf).reshape(dgu_ref.shape[1:])
+    ddn_ref[...] = dot_tl(h, g).astype(bf)
+    @pl.when(j == steps - 1)
+    def _():
+        total = jnp.zeros((1, d), f32)
+        for t in range(0, R, CH):
+            s = slice(t, t + CH)
+            out_ref[s, :] = acc[s, :].astype(bf)
+            y = res[s, :]
+            r = lax.rsqrt(jnp.mean(y * y, axis=-1, keepdims=True) + EPS)
+            m = y * r
+            gn = gres_ref[s, :]
+            total = total + jnp.sum(gn * m, axis=0, keepdims=True)
+            w = gn * gain_ref[0:1, :]
+            gr = g_ref[s, :].astype(f32) + r * (w - m * jnp.mean(w * m, axis=-1, keepdims=True))
+            gres_ref[s, :] = gr
+            low = gr.astype(bf)
+            n[s, :] = low
+            gctx_ref[s, :] = dot_nt(low, wo_ref[...]).astype(bf)
+        ggain_ref[...] = jnp.broadcast_to(total, ggain_ref.shape)
+        dwo_ref[...] = dot_tl(ctx_ref[...], n[...]).astype(bf)
+
+def ffn(x, ctx, g, gain, wo, gu, dn, block=256):
+    R, d = x.shape
+    F = dn.shape[0]
+    k = gu.shape[1]
+    sds = jax.ShapeDtypeStruct
+    one = lambda *s: pl.BlockSpec(s, lambda j: (0,) * len(s), pipeline_mode=pl.Buffered(1))
+    gub = pl.BlockSpec((2, k, d // k, block), lambda j: (0, 0, 0, j))
+    dnb = pl.BlockSpec((block, d), lambda j: (j, 0))
+    return pl.pallas_call(ffn_kernel, grid=(F // block,),
+        in_specs=[one(R, d), one(R, d), one(R, d), one(1, d), one(d, d), gub, dnb],
+        out_specs=[one(R, d), one(R, d), one(R, d), one(d, d), one(8, d), gub, dnb],
+        out_shape=[sds((R, d), bf), sds((R, d), f32), sds((R, d), bf), sds((d, d), bf), sds((8, d), f32), sds(gu.shape, bf), sds(dn.shape, bf)],
+        scratch_shapes=[pltpu.VMEM((R, d), f32), pltpu.VMEM((R, d), bf), pltpu.VMEM((R, d), f32)],
+        compiler_params=pltpu.CompilerParams(vmem_limit_bytes=61 * 2**20), name="ffn")(x, ctx, g, gain, wo, gu, dn)
+
+def contract_rows(left, right):
+    return lax.dot_general(left, right, (((0,), (0,)), ((), ())), preferred_element_type=f32)
+
+def contract_cols(left, right):
+    return lax.dot_general(left, right, (((1,), (1,)), ((), ())), preferred_element_type=f32)
 
 def rms_norm(inputs, gain):
     return inputs * lax.rsqrt(jnp.mean(inputs * inputs, axis=-1, keepdims=True) + EPS) * gain
 
-def gated(gate_in, up_in):
-    return jax.nn.gelu(gate_in, approximate=True) * up_in
-
-def contract_rows(left, right):
-    return lax.dot_general(left, right, (((0,), (0,)), ((), ())), preferred_element_type=f32)
-
-def contract_cols(left, right):
-    return lax.dot_general(left, right, (((1,), (1,)), ((), ())), preferred_element_type=f32)
-
 def gather(x):
-    return lax.all_gather(x, SHARD, axis=0, tiled=True)
+    return lax.all_gather(x, SHARD, axis=0, tiled=False)
 
 def scatter(x):
     return lax.psum_scatter(x, SHARD, scatter_dimension=0, tiled=True)
 
-def per_device(tokens, row_kind, text_length, gain_attn, position_bias_table, weight_query, weight_key, weight_value, weight_out, gain_ffn, weight_gate, weight_up, weight_down, cotangent):
-    small = lax.all_gather(jnp.concatenate([gain_attn, gain_ffn, position_bias_table]), SHARD, axis=0, tiled=False)
-    qkv_w = gather(jnp.concatenate([weight_query, weight_key, weight_value], 1))
-    gu_w = gather(jnp.concatenate([weight_out, weight_gate, weight_up], 1))
-    down_w = gather(weight_down)
-    d = qkv_w.shape[0]
-    ff = weight_gate.shape[1]
-    n1 = gain_attn.shape[0]
-    gain_one = small[:, :n1].reshape(d).astype(f32)
-    gain_two = small[:, n1:2 * n1].reshape(d).astype(f32)
-    table = small[:, 2 * n1:].reshape(-1)
-    far, w = tables(table)
+def per_device(near, tokens, row_kind, text_length, gain_attn, position_bias_table, weight_query, weight_key, weight_value, weight_out, gain_ffn, weight_gate, weight_up, weight_down, cotangent):
+    n1, d = weight_query.shape
+    n2 = position_bias_table.shape[0]
+    gu_shard = jnp.stack([weight_gate, weight_up])
     mask = mask_cols(row_kind, text_length)
     inputs = tokens.astype(f32)
-    normed = rms_norm(inputs, gain_one).astype(bf)
-    q = dot(normed, qkv_w[:, :d]).astype(bf)
-    k = dot(normed, qkv_w[:, d:2 * d]).astype(bf)
-    v = dot(normed, qkv_w[:, 2 * d:]).astype(bf)
-    context, e, r = attn_fwd(q, k, v, mask, far, w)
-    out_w, gate_w, up_w = gu_w[:, :d], gu_w[:, d:d + ff], gu_w[:, d + ff:]
-    residual = inputs + dot(context, out_w)
-    normed_ffn = rms_norm(residual, gain_two).astype(bf)
-    gate_pre = dot(normed_ffn, gate_w)
-    up_pre = dot(normed_ffn, up_w)
-    hidden = gated(gate_pre, up_pre).astype(bf)
-    output = (residual + dot(hidden, down_w)).astype(bf)
-    grad_output = cotangent.astype(f32)
-    grad_down = contract_rows(hidden, cotangent).astype(bf)
-    s_down = scatter(grad_down)
-    grad_hidden = contract_cols(cotangent, down_w)
-    _, gate_pull = jax.vjp(gated, gate_pre, up_pre)
-    gg, gu = gate_pull(grad_hidden)
-    gg = gg.astype(bf)
-    gu = gu.astype(bf)
-    grad_normed_ffn = contract_cols(gg, gate_w) + contract_cols(gu, up_w)
-    gw_gate = contract_rows(normed_ffn, gg).astype(bf)
-    gw_up = contract_rows(normed_ffn, gu).astype(bf)
-    _, norm_pull = jax.vjp(rms_norm, residual, gain_two)
-    part, g_gain_two = norm_pull(grad_normed_ffn)
-    grad_residual = grad_output + part
-    gr_low = grad_residual.astype(bf)
-    grad_out_w = contract_rows(context, gr_low).astype(bf)
-    s_gu = scatter(jnp.concatenate([grad_out_w, gw_gate, gw_up], 1))
-    grad_context = contract_cols(gr_low, out_w).astype(bf)
-    gq, gk, gv, near, farsum = attn_bwd(q, k, v, grad_context, context, r, e)
-    g_table = table_grad(near, farsum)
-    gqkv = jnp.concatenate([contract_rows(normed, x).astype(bf) for x in (gq, gk, gv)], 1)
-    s_qkv = scatter(gqkv)
-    grad_normed = contract_cols(gq, qkv_w[:, :d]) + contract_cols(gk, qkv_w[:, d:2 * d]) + contract_cols(gv, qkv_w[:, 2 * d:])
+    if near:
+        small = jnp.pad(jnp.stack([gain_attn, gain_ffn, jnp.pad(position_bias_table, (0, n1 - n2))]), ((0, n1 - 3), (0, 0)))
+        q, k, v, normed, qkv_w = gather_qkv(tokens, small, weight_query, weight_key, weight_value)
+        small = qkv_w[:, 0:3, 3 * d:]
+        gain_one = small[:, 0].reshape(d).astype(f32)
+    else:
+        small = gather(jnp.stack([gain_attn, gain_ffn, jnp.pad(position_bias_table, (0, n1 - n2))]))
+        qkv_w = gather(jnp.concatenate([weight_query, weight_key, weight_value], 1))
+        gain_one = small[:, 0].reshape(d).astype(f32)
+        normed = rms_norm(inputs, gain_one).astype(bf)
+        q, k, v = (dot(normed, qkv_w[:, :, t * d:t * d + d].reshape(d, d)).astype(bf) for t in range(3))
+    gain_two = small[:, 1].reshape(d).astype(f32)
+    far, w = tables(small[:, 2, :n2].reshape(-1))
+    if near:
+        context, e, r, gu_w, down_w, out_w = attn_fwd_gather(q, k, v, mask, far, w, gu_shard, weight_down, weight_out)
+    else:
+        context, e, r = attn_fwd(q, k, v, mask, far, w)
+        gu_w, down_w, out_w = jnp.moveaxis(gather(gu_shard), 0, 1), gather(weight_down), gather(weight_out)
+    ff = gu_w.shape[-1]
+    output, grad_residual, grad_context, grad_out_w, g_gain_two, dgu, ddn = ffn(
+        tokens, context, cotangent, gain_two.reshape(1, d), out_w.reshape(d, d), gu_w, down_w.reshape(ff, d))
+    g_gain_two = g_gain_two[0]
+    s_gu = jnp.stack([scatter(dgu[0].reshape(d, ff)), scatter(dgu[1].reshape(d, ff))])
+    s_down = scatter(ddn)
+    s_out = scatter(grad_out_w)
+    gq, gk, gv, near_sums, far_sums = attn_bwd(q, k, v, grad_context, context, r, e)
+    g_table = table_grad(near_sums, far_sums)
+    grads = (gq, gk, gv)
+    s_qkv = scatter(jnp.concatenate([contract_rows(normed, x).astype(bf) for x in grads], 1))
+    grad_normed = sum(contract_cols(x, qkv_w[:, :, t * d:t * d + d].reshape(d, d)) for t, x in enumerate(grads))
     _, first_pull = jax.vjp(rms_norm, inputs, gain_one)
     share, g_gain_one = first_pull(grad_normed)
     grad_tokens = grad_residual + share
-    small_g = jnp.concatenate([g_gain_one, g_gain_two, g_table])
-    small_g = lax.psum(small_g, ("batch", "dp", "narrow"))
+    small_g = lax.psum(jnp.concatenate([g_gain_one, g_gain_two, g_table]), ("batch", "dp", "narrow"))
     at = lax.axis_index("dp") * lax.axis_size("narrow") + lax.axis_index("narrow")
-    n2 = position_bias_table.shape[0]
     r_gain_one = lax.dynamic_slice_in_dim(small_g, at * n1, n1)
     r_gain_two = lax.dynamic_slice_in_dim(small_g, d + at * n1, n1)
     r_table = lax.dynamic_slice_in_dim(small_g, 2 * d + at * n2, n2)
-    ar = lambda x: lax.psum(x, "batch").astype(f32)
-    s_gu, s_down, s_qkv = ar(s_gu), ar(s_down), ar(s_qkv)
-    return (output, grad_tokens, r_gain_one, r_table, s_qkv[:, :d], s_qkv[:, d:2 * d], s_qkv[:, 2 * d:], s_gu[:, :d], r_gain_two, s_gu[:, d:d + ff], s_gu[:, d + ff:], s_down)
+    s_gu, s_down, s_out, s_qkv = (lax.psum(x, "batch").astype(f32) for x in (s_gu, s_down, s_out, s_qkv))
+    return (output, grad_tokens, r_gain_one, r_table, s_qkv[:, :d], s_qkv[:, d:2 * d], s_qkv[:, 2 * d:], s_out, r_gain_two, s_gu[0], s_gu[1], s_down)
 
 def solution(mesh):
+    near = (mesh.shape["batch"], mesh.shape["dp"], mesh.shape["narrow"]) == (4, 4, 2)
     placed = (
         P(("batch", "dp", "narrow"), None),
         P(("batch", "dp", "narrow")),
@@ -291,7 +558,7 @@
         P(("batch", "dp", "narrow"), None),
     )
     return jax.shard_map(
-        per_device,
+        functools.partial(per_device, near),
         mesh=mesh,
         in_specs=placed,
         out_specs=(

time: 739 us -> 699 us (0.946)
  Pallas kernels: 104 us -> 283 us
  matrix products: 190 us -> 28.8 us
  waiting for transfers between devices: 268 us -> 245 us
  blocking collectives: 59.2 us -> 42.9 us
  other arithmetic: 43.3 us -> 34.8 us
  local copies, waits for them, and re-layouts: 48.4 us -> 41 us
    pallas_call x1 -> x3, Pallas kernels: 43.1 us -> 221 us  [the longest x1 98.5 us: ffn(): pl.pallas_call(ffn_kernel, grid=(F // block,), in_specs=[one(R, d), one(R...]
    dot_general x7 -> x0, matrix products: 71.6 us -> none  [dot(): return jnp.dot(a, b, preferred_element_type=f32)]
    all_gather x3 -> x0, waiting for transfers between devices: 66.3 us -> none  [gather(): return lax.all_gather(x, SHARD, axis=0, tiled=True)]
    unnamed x8 -> x7, waiting for transfers between devices: 0.8 us -> 64.3 us
    dot_general x7 -> x3, matrix products: 63 us -> 17 us  [contract_cols(): lax.dot_general(left, right, (((1,), (1,)), ((), ())), preferred_element_...]
    dot_general x7 -> x3, matrix products: 55.2 us -> 11.4 us  [contract_rows(): lax.dot_general(left, right, (((0,), (0,)), ((), ())), preferred_element_...]
    reduce_scatter x2 -> x4, waiting for transfers between devices: 145 us -> 115 us  [scatter(): return lax.psum_scatter(x, SHARD, scatter_dimension=0, tiled=True)]
    unnamed x68 -> x43, local copies, waits for them, and re-layouts: 33.6 us -> 14.3 us
  transfers between devices with their start and end apart: 7 -> 6, of which waited for: 6 -> 5; matrix products, arithmetic and copies ran while one was open for 21% -> 11% of each run, Pallas kernels for 6% -> 9%
where the time goes in v2:
time: 699 us; the launch traced here: 691 us
  Pallas kernels  283 us (40%)
  waiting for transfers between devices  245 us (35%)
  blocking collectives  42.9 us (6%)
  local copies, waits for them, and re-layouts  41 us (6%)
  other arithmetic  34.8 us (5%)
  matrix products  28.8 us (4%)
  between operations  15.6 us (2%)
    reduce_scatter x4, waiting for transfers between devices, scatter(): return lax.psum_scatter(x, SHARD, scatter_dimension=0, tiled=True)  115 us
    pallas_call x1, Pallas kernels, ffn(): pl.pallas_call(ffn_kernel, grid=(F // block,), in_specs=[one(R, d), one(R...  98.5 us
    pallas_call x1, Pallas kernels, attn_fwd_gather(): pl.pallas_call(fwd_gather_kernel, grid=(rows, 8), in_specs=[spec, spec, s...  81.1 us
    psum x1, waiting for transfers between devices, per_device(): lax.psum(x, 'batch').astype(f32)  66 us
    unnamed x7, waiting for transfers between devices  64.3 us
    pallas_call x1, Pallas kernels, attn_bwd(): pl.pallas_call(bwd_kernel, grid=(rows, 8), in_specs=[spec] * 6 + [pl.Bloc...  61.4 us
    psum x1, blocking collectives, per_device(): lax.psum(jnp.concatenate([g_gain_one, g_gain_two, g_table]), ('batch', 'd...  42.9 us
    pallas_call x1, Pallas kernels, gather_qkv(): pl.pallas_call(qkv_kernel, in_specs=[vm] * 5, out_specs=[vm] * 4 + [pl.Bl...  41.5 us
  transfers between devices with their start and end apart: 6, of which 5 were waited for; matrix products, arithmetic and copies ran while one was open for 11% of the time, Pallas kernels for 9%

profile of v2, /device:TPU:0, one launch (start us, length us, event | category | flops | bytes accessed | tf_op | source)
XLA Modules:
  0.0 691.3 jit_solution(1906504291621277707)
XLA Ops:
  7.3 0.8 pad_bitcast_fusion
  8.1 1.3 fusion.10.small_ref
  9.4 41.5 %gather_qkv.1 = (bf16[1152,1024]{1,0:T(8,128)(2,1)}, bf16[1152,1024]{1,0:T(8,128)(2,1)}, bf16[1152,1024]{1,0:T(8,128)(2,1)}, bf16[1152,1024]{1,0:T(8,128)(2,1)}, bf16[8,128,3200]{2,1,0:T(8,128)(2,1)}) custom-call(bf16[1152,1024]{1,0:T(8,128)(2,1)} %x_ref.3, bf16[128,128]{1,0:T(8,128)(2,1)} %fusion.10.small_ref, bf16[128,1024]{1,0:T(8,128)(2,1)} %wq_ref.1, ...), custom_call_target="tpu_custom_call" | custom-call | tf_op jit(solution)/shard_map/gather_qkv/pallas_call | solution.py:280
  50.9 0.7 slice_reduce_fusion.2
  51.6 0.7 convert_reduce_fusion
  52.4 1.4 slice_convert_fusion
  54.4 0.6 fusion.21
  55.2 0.2 slice_reduce_fusion.1
  55.3 0.1 tile.20
  55.4 0.1 copy.53
  55.6 0.1 copy.55
  55.7 0.2 fusion.14
  56.1 1.2 pad_maximum_fusion.1.refs_6_
  57.3 0.6 select_maximum_fusion.refs_4_
  58.0 0.7 pad.19.refs_5_
  58.6 2.0 compare_reduce_fusion
  60.6 1.8 and_select_fusion.refs_3_
  62.4 81.1 %attn_fwd_gather.1 = (bf16[1152,1024]{1,0:T(8,128)(2,1)}, bf16[1,8,1152,2304]{3,2,1,0:T(8,128)(2,1)}, f32[1152,1024]{1,0:T(8,128)}, bf16[2,8,128,2816]{3,2,1,0:T...) custom-call(bf16[1152,1024]{1,0:T(8,128)(2,1)} %get-tuple-element.35.refs_0_.q_ref, ...), custom_call_target="tpu_custom_call" | custom-call | tf_op jit(solution)/shard_map/attn_fwd_gather/pallas_call | solution.py:390
  143.6 98.5 %ffn.1 = (bf16[1152,1024]{1,0:T(8,128)(2,1)}, f32[1152,1024]{1,0:T(8,128)}, bf16[1152,1024]{1,0:T(8,128)(2,1)}, bf16[1024,1024]{1,0:T(8,128)(2,1)}, f32[8,1024]{...) custom-call(bf16[1152,1024]{1,0:T(8,128)(2,1)} %x_ref.3, ...), custom_call_target="tpu_custom_call" | custom-call | tf_op jit(solution)/shard_map/ffn/pallas_call | solution.py:473
  242.1 9.6 %fusion.16 = (bf16[1,8,128,2816]{3,2,1,0:T(8,128)(2,1)}, bf16[1,8,128,2816]{3,2,1,0:T(8,128)(2,1)}) fusion(bf16[2,8,128,2816]{3,2,1,0:T(8,128)(2,1)} %get-tuple-element.56), kind=kLoop, calls=%fused_computation.51 | loop fusion | bytes 23068672 | tf_op jit(solution)/shard_map/slice | solution.py:523
  251.8 0.7 reduce-scatter.10.cloned.1.call-update
  252.5 61.4 %attn_bwd.1 = (bf16[1152,1024]{1,0:T(8,128)(2,1)}, bf16[1152,1024]{1,0:T(8,128)(2,1)}, bf16[1152,1024]{1,0:T(8,128)(2,1)}, f32[1,8,8,512]{3,2,1,0:T(8,128)}, f32[1,8,8,128]{3,2,1,0:T(8,128)}) custom-call(bf16[1152,1024]{1,0:T(8,128)(2,1)} %get-tuple-element.35.refs_0_.q_ref, bf16[1152,1024]{1,0:T(8,128)(2,1)} %get-tuple-element.36.refs_1_.k_ref, ...), custom_call_target="tpu_custom_call" | custom-call | tf_op jit(solution)/shard_map/attn_bwd/pallas_call | solution.py:177
  314.0 5.0 convolution_convert_fusion.2
  319.0 3.2 convolution_convert_fusion.1
  322.2 3.2 convolution_convert_fusion
  325.4 13.4 %pad_maximum_fusion = bf16[1024,3072]{0,1:T(8,128)(2,1)} fusion(bf16[1024,1024]{0,1:T(8,128)(2,1)S(1)} %convolution_convert_fusion, bf16[1024,1024]{0,1:T(8,128)(2,1)S(1)} %convolution_convert_fusion.1, bf16[1024,1024]{0,1:T(8,128)(2,1)S(1)} %convolution_convert_fusion.2), kind=kLoop, calls=%fused_computation.5 | loop fusion | flops 18874368 | bytes 12582912 | tf_op jit(solution)/shard_map/concatenate | solution.py:529
  338.7 9.0 %copy.66 = bf16[1024,3072]{1,0:T(8,128)(2,1)} copy(bf16[1024,3072]{0,1:T(8,128)(2,1)} %pad_maximum_fusion) | data formatting | bytes 12582912
  347.8 0.5 reduce-scatter.8.cloned.1.call-update
  348.4 0.5 reduce-scatter.14.cloned.1.call-update
  348.9 1.2 slice.85
  350.1 0.8 slice.84
  350.9 0.8 slice.86
  351.7 0.1 copy.60
  351.8 0.1 reduce_sum.41
  351.9 0.1 copy.61
  352.0 0.1 mul.140
  352.1 0.1 copy.62
  352.1 0.1 mul.145
  352.2 0.2 fusion.5
  352.5 0.1 reshape.228
  352.6 0.5 fusion.1
  353.1 6.1 fusion.17
  359.2 4.6 fusion.22
  363.8 10.3 %reduce-scatter.10.cloned.1.call-done = bf16[128,2816]{1,0:T(8,128)(2,1)} async-done(((bf16[1024,2816]{1,0:T(8,128)(2,1)}), bf16[128,2816]{1,0:T(8,128)(2,1)}) %reduce-scatter.10.cloned.1.call-update) | async-done | bytes 720912 | tf_op jit(solution)/shard_map/reduce_scatter | solution.py:493
  374.1 2.6 pad_maximum_fusion.2
  376.6 62.6 %reduce-scatter.16.cloned.1.call-done = bf16[128,3072]{1,0:T(8,128)(2,1)} async-done(((bf16[1024,3072]{1,0:T(8,128)(2,1)}), bf16[128,3072]{1,0:T(8,128)(2,1)}) %reduce-scatter.16.cloned.1.call-update) | async-done | bytes 786448
  439.2 2.3 copy.67
  441.5 42.5 %reduce-scatter.8.cloned.1.call-done = bf16[128,1024]{1,0:T(8,128)(2,1)} async-done(((bf16[1024,1024]{1,0:T(8,128)(2,1)}), bf16[128,1024]{1,0:T(8,128)(2,1)}) %reduce-scatter.8.cloned.1.call-update) | async-done | bytes 262160 | tf_op jit(solution)/shard_map/reduce_scatter | solution.py:493
  484.0 62.4 %reduce-scatter.14.cloned.1.call-done = bf16[352,1024]{1,0:T(8,128)(2,1)} async-done(((bf16[2816,1024]{1,0:T(8,128)(2,1)}), bf16[352,1024]{1,0:T(8,128)(2,1)}) %reduce-scatter.14.cloned.1.call-update) | async-done | bytes 720912 | tf_op jit(solution)/shard_map/reduce_scatter | solution.py:493
  546.4 5.1 fusion.23
  551.5 7.3 %fusion.4 = (f32[1024]{0:T(1024)S(1)}, f32[1152]{0:T(1024)S(1)}, f32[1152,1024]{1,0:T(8,128)}) fusion(bf16[1152,1024]{1,0:T(8,128)(2,1)S(1)} %copy-done, f32[1152]{0:T(1024)S(1)} %fusion.11, f32[1024]{0:T(1024)S(1)} %bitcast.72, bf16[1152,1024]{1,0:T(8,128)(2,1)S(1)} %copy-done.3, bf16[1024,1024]{1,0:T(8,128)(2,1)S(1)} %bitcast.60, ...), kind=kOutput, calls=%fused_computation.10 | convolution fusion | flops 2426533888 | bytes 20988928 | tf_op jit(solution)/shard_map/dot_general | solution.py:484
  558.9 42.9 %psum.35 = f32[2560]{0:T(1024)S(1)} all-reduce(f32[2560]{0:T(1024)S(1)} %pad_maximum_fusion.3), channel_id=1, replica_groups=mesh['batch'=4,'dp'=4,'narrow'=2] {'batch','dp','narrow'}, use_global_device_ids=true, to_apply=%region_4.5 | all-reduce | flops 2560 | bytes 20480 | tf_op jit(solution)/shard_map/psum | solution.py:534
  601.8 0.6 dynamic_slice.10
  602.4 0.6 fusion.19
  603.0 5.9 fusion
  608.9 66.0 %all-reduce.7.cloned.1.call-done = (bf16[128,3072]{0,1:T(8,128)(2,1)}, bf16[128,1024]{1,0:T(8,128)(2,1)}, bf16[2,128,2816]{2,1,0:T(8,128)(2,1)}, bf16[352,1024]{1,0:T(8,128)(2,1)}) async-done(((bf16[128,3072]{0,1:T(8,128)(2,1)}, bf16[128,1024]{1,0:T(8,128)(2,1)}, bf16[2,128,2816]{2,1,0:T(8,128)(2,1)}, bf16[352,1024]{1,0:T(8,128)(2,1)}), (bf16[128,3072]{0,1:T(8,128)(2,1)}, bf16[128,1024]{1,0:T(8,128)(2,1)}, ...) | async-done | bytes 3211280 | tf_op jit(solution)/shard_map/psum | solution.py:539
  674.8 1.8 convert_element_type.72
  676.6 1.2 fusion.18
  677.8 1.0 copy.65
  678.8 1.0 copy.64
  679.8 1.0 copy.63
  680.8 1.3 convert_element_type.74
  682.1 0.2 convert_element_type.73
  682.3 1.8 slice_bitcast_fusion
  (63 shorter events, 0.9 us)
Async XLA Ops:
  7.2 48.5 %copy-start.9 = (f32[32,512,1]{1,0,2:T(8,128)S(1)}, f32[32,512,1]{1,0,2:T(8,128)}, u32[]{:S(2)}) copy-start(f32[32,512,1]{1,0,2:T(8,128)} %constant.89) | copy-start | bytes 196612
  7.2 48.8 %copy-start.18 = (s32[1,128]{1,0:T(1,128)S(1)}, s32[1,128]{1,0:T(1,128)}, u32[]{:S(2)}) copy-start(s32[1,128]{1,0:T(1,128)} %constant.72.clone) | copy-start | bytes 1540
  7.2 48.8 %copy-start.10 = (s32[1,1152]{1,0:T(1,128)S(1)}, s32[1,1152]{1,0:T(1,128)}, u32[]{:S(2)}) copy-start(s32[1,1152]{1,0:T(1,128)} %constant.70.clone) | copy-start | bytes 13828
  7.2 47.2 %copy-start.12 = (s32[1,3]{1,0:T(1,128)S(1)}, s32[1,3]{1,0:T(1,128)}, u32[]{:S(2)}) copy-start(s32[1,3]{1,0:T(1,128)} %param.23) | copy-start | bytes 40
  7.2 48.9 %copy-start.6 = (bf16[128,2816]{1,0:T(8,128)(2,1)S(1)}, bf16[128,2816]{1,0:T(8,128)(2,1)}, u32[]{:S(2)}) copy-start(bf16[128,2816]{1,0:T(8,128)(2,1)} %param.32) | copy-start | bytes 2162692
  7.2 48.9 %copy-start.7 = (bf16[128,2816]{1,0:T(8,128)(2,1)S(1)}, bf16[128,2816]{1,0:T(8,128)(2,1)}, u32[]{:S(2)}) copy-start(bf16[128,2816]{1,0:T(8,128)(2,1)} %param.31) | copy-start | bytes 2162692
  7.2 356.6 %reduce-scatter.12.cloned.1.call-start = ((), (), s32[]{:S(2)}) async-start(), calls=%async_computation.7 | async-start | bytes 6488064 | tf_op jit(solution)/shard_map/reduce_scatter | solution.py:493
  50.9 7.8 %copy-start.11 = (s32[1,1152]{1,0:T(1,128)S(1)}, s32[1,1152]{1,0:T(1,128)}, u32[]{:S(2)}) copy-start(s32[1,1152]{1,0:T(1,128)} %constant.71.clone) | copy-start | bytes 13828
  251.7 122.4 %reduce-scatter.10.cloned.1.call-start = ((), (), s32[]{:S(2)}) async-start(), calls=%async_computation.6 | async-start | bytes 6488064 | tf_op jit(solution)/shard_map/reduce_scatter | solution.py:493
  252.5 186.8 %reduce-scatter.16.cloned.1.call-start = ((), (), s32[]{:S(2)}) async-start(), calls=%async_computation.9 | async-start | bytes 7077888
  252.5 61.4 %copy-start.17 = (bf16[1152,1024]{1,0:T(8,128)(2,1)S(1)}, bf16[1152,1024]{1,0:T(8,128)(2,1)}, u32[]{:S(2)}) copy-start(bf16[1152,1024]{1,0:T(8,128)(2,1)} %get-tuple-element.54) | copy-start | bytes 7077892
  313.9 5.0 copy-start.15
  319.0 3.2 copy-start.2
  347.7 136.2 %reduce-scatter.8.cloned.1.call-start = ((), (), s32[]{:S(2)}) async-start(), calls=%async_computation.5 | async-start | bytes 2359296 | tf_op jit(solution)/shard_map/reduce_scatter | solution.py:493
  348.3 198.0 %reduce-scatter.14.cloned.1.call-start = ((), (), s32[]{:S(2)}) async-start(), calls=%async_computation.8 | async-start | bytes 6488064 | tf_op jit(solution)/shard_map/reduce_scatter | solution.py:493
  348.3 3.9 copy-start.8
  348.4 3.9 copy-start.13
  348.4 3.9 copy-start.14
  348.4 4.2 copy-start
  348.9 325.9 %all-reduce.7.cloned.1.call-start = ((), (), s32[]{:S(2)}) async-start(), calls=%async_computation.10 | async-start | bytes 6422528 | tf_op jit(solution)/shard_map/psum | solution.py:539
  353.1 6.1 copy-start.16
  546.3 5.1 copy-start.1
  546.4 5.1 copy-start.3
  677.8 3.0 copy-start.5
  678.8 3.3 copy-start.4
Sparse Core Ops, SparseCore 0:
  251.8 59.2 reduce-scatter.11
  315.0 59.0 reduce-scatter.9
  377.5 61.7 reduce-scatter.15
  442.7 41.2 reduce-scatter.7
  487.2 59.0 reduce-scatter.13
  549.6 125.2 all-reduce.6
